TPU v7x, 512 devices: a whole 4x4x16 slice. The times are simulated.
512 devices in a mesh: member: 4 (over y_hi, core), lat: 8 (over x, y_lo), lon: 16 (over z).
Axes of the slice: x: 4, y: 4 (y_hi: 2, y_lo: 2; y = y_hi * 2 + y_lo), z: 16, core: 2. Of those that a mesh axis runs over, the one named last changes fastest.
Arguments:
- fields: bfloat16 [12, 128, 128, 256], P('member', 'lat', 'lon'), may hold values from -6 to 6
- land_mask: int32 [128, 128], P('lat', 'lon'), may hold values 0 or 1
- offsets: int32 [2], replicated, may hold values from 1 to 7
- land_embed: float32 [256], replicated, may hold values from -5 to 5
- win_qkv: bfloat16 [256, 768], replicated, may hold values from -16 to 16, as said below
- win_out: bfloat16 [256, 256], replicated, may hold values from -0.375 to 0.375
- win_up: bfloat16 [256, 1024], replicated, may hold values from -0.375 to 0.375
- win_down: bfloat16 [1024, 256], replicated, may hold values from -0.1875 to 0.1875
- mem_qkv: bfloat16 [256, 768], replicated, may hold values from -16 to 16, as said below
- mem_out: bfloat16 [256, 256], replicated, may hold values from -0.375 to 0.375
- shift_qkv: bfloat16 [256, 768], replicated, may hold values from -16 to 16, as said below
- shift_out: bfloat16 [256, 256], replicated, may hold values from -0.375 to 0.375
- shift_up: bfloat16 [256, 1024], replicated, may hold values from -0.375 to 0.375
- shift_down: bfloat16 [1024, 256], replicated, may hold values from -0.1875 to 0.1875
Outputs:
- updated: bfloat16 [12, 128, 128, 256], P('member', 'lat', 'lon')
Inputs may be any that keep to these rules, and one draw needn't show every extreme that they name: `win_qkv`: query, key and value projection: columns 0 to 255 are queries, then keys, then values, each in 4 heads of 64. `mem_qkv`: laid out as win_qkv. `shift_qkv`: laid out as win_qkv.
All inputs are finite; a program needn't handle non-finite values. No bound on the sum of `land_mask` on one device may be relied on, other than what follows from the above.
Results may differ from a plain program's by a relative error of at most 0.013.
Values may be sent and summed in bfloat16 or wider, within the bound.
A program may use at most 64 MiB of HBM per device.

v0:
```python
import jax
import jax.numpy as jnp
from jax import lax
from jax.sharding import PartitionSpec as P

HEADS = 4
WIN = 8


epsilon = 1e-05


def with_halo(block, sides, width):
    for axis, dim in sides:
        count = lax.axis_size(axis)
        forward = [(i, i + 1) for i in range(count - 1)]
        forward.append((count - 1, 0))
        backward = [(target, source) for source, target in forward]
        low = lax.ppermute(
            lax.slice_in_dim(block, block.shape[dim] - width, None, axis=dim), axis, forward
        )
        high = lax.ppermute(lax.slice_in_dim(block, 0, width, axis=dim), axis, backward)
        block = jnp.concatenate([low, block, high], axis=dim)
    return block


def normalize(stream):
    average = jnp.mean(stream, axis=-1, keepdims=True)
    centered = stream - average
    spread = jnp.mean(centered * centered, axis=-1, keepdims=True)
    return (centered * lax.rsqrt(spread + epsilon)).astype(jnp.bfloat16)


def project(inputs, matrix):
    flattened = inputs.reshape(-1, inputs.shape[-1])
    result = jnp.dot(flattened, matrix, preferred_element_type=jnp.float32)
    return result.reshape(inputs.shape[:-1] + (matrix.shape[1],))


def to_windows(tensor):
    height, breadth, channels = tensor.shape
    tensor = tensor.reshape(height // WIN, WIN, breadth // WIN, WIN, channels)
    return tensor.transpose(0, 2, 1, 3, 4).reshape(
        height // WIN, breadth // WIN, WIN * WIN, channels
    )


def from_windows(tensor, height, breadth):
    channels = tensor.shape[-1]
    tensor = tensor.reshape(height // WIN, breadth // WIN, WIN, WIN, channels).transpose(
        0, 2, 1, 3, 4
    )
    return tensor.reshape(height, breadth, channels)


def plain_windows(qkv_rows):
    height, breadth, triple = qkv_rows.shape
    channels = triple // 3
    head_size = channels // HEADS
    blocks = to_windows(qkv_rows)
    split_heads = blocks.reshape(blocks.shape[:3] + (3, HEADS, head_size))
    scores = jnp.einsum(
        "abqhe,abkhe->abhqk",
        split_heads[:, :, :, 0],
        split_heads[:, :, :, 1],
        preferred_element_type=jnp.float32,
    ) * head_size ** (-0.5)
    weights = jax.nn.softmax(scores, axis=-1).astype(jnp.bfloat16)
    result = jnp.einsum(
        "abhqk,abkhe->abqhe", weights, split_heads[:, :, :, 2], preferred_element_type=jnp.float32
    ).astype(jnp.bfloat16)
    return from_windows(result.reshape(blocks.shape[:3] + (channels,)), height, breadth)


def feed_forward(stream, w_up, w_down):
    hidden = jax.nn.gelu(project(normalize(stream), w_up), approximate=False).astype(jnp.bfloat16)
    return stream + project(hidden, w_down)


def member_attention(qkv_rows):
    members, ignored, amount, triple = qkv_rows.shape
    channels = triple // 3
    head_size = channels // HEADS
    split_heads = qkv_rows.reshape(members, amount, 3, HEADS, head_size)
    scores = jnp.einsum(
        "mthe,nthe->thmn",
        split_heads[:, :, 0],
        split_heads[:, :, 1],
        preferred_element_type=jnp.float32,
    ) * head_size ** (-0.5)
    weights = jax.nn.softmax(scores, axis=-1).astype(jnp.bfloat16)
    result = jnp.einsum(
        "thmn,nthe->mthe", weights, split_heads[:, :, 2], preferred_element_type=jnp.float32
    ).astype(jnp.bfloat16)
    return result.reshape(members, 1, amount, channels)


def shifted_attention(queries, borders, offsets, lat_first, lon_first, lat_total, lon_total):
    members, height, breadth, channels = queries.shape
    margin = (borders.shape[1] - height) // 2
    head_size = channels // HEADS
    q_rows = lat_first + jnp.arange(height, dtype=jnp.int32)
    q_cols = lon_first + jnp.arange(breadth, dtype=jnp.int32)
    k_rows = lat_first - margin + jnp.arange(height + 2 * margin, dtype=jnp.int32)
    k_cols = (lon_first - margin + jnp.arange(breadth + 2 * margin, dtype=jnp.int32)) % lon_total
    q_lat = jnp.floor_divide(q_rows - offsets[0], WIN)
    inside = (k_rows >= 0) & (k_rows < lat_total)
    k_lat = jnp.where(inside, jnp.floor_divide(k_rows - offsets[0], WIN), -1000)
    q_lon = jnp.floor_divide((q_cols - offsets[1]) % lon_total, WIN)
    k_lon = jnp.floor_divide((k_cols - offsets[1]) % lon_total, WIN)
    allowed = (q_lat[:, None, None, None] == k_lat[None, None, :, None]) & (
        q_lon[None, :, None, None] == k_lon[None, None, None, :]
    )
    allowed = allowed.reshape(height * breadth, -1)
    query_heads = queries.reshape(members, height * breadth, HEADS, head_size)
    key_heads = borders[..., :channels].reshape(members, -1, HEADS, head_size)
    value_heads = borders[..., channels:].reshape(members, -1, HEADS, head_size)

    def attend_member(operands):
        query_part, key_part, value_part = operands
        scores = jnp.einsum(
            "qhe,khe->hqk", query_part, key_part, preferred_element_type=jnp.float32
        ) * head_size ** (-0.5)
        scores = jnp.where(allowed[None], scores, -1e30)
        weights = jax.nn.softmax(scores, axis=-1).astype(jnp.bfloat16)
        return jnp.einsum(
            "hqk,khe->qhe", weights, value_part, preferred_element_type=jnp.float32
        ).astype(jnp.bfloat16)

    result = lax.map(attend_member, (query_heads, key_heads, value_heads))
    return result.reshape(members, height, breadth, channels)


def per_device(
    fields,
    land_mask,
    offsets,
    land_embed,
    win_qkv,
    win_out,
    win_up,
    win_down,
    mem_qkv,
    mem_out,
    shift_qkv,
    shift_out,
    shift_up,
    shift_down,
):
    members, height, breadth, channels = fields.shape
    stream = (
        fields.astype(jnp.float32)
        + land_mask.astype(jnp.float32)[None, :, :, None] * land_embed[None, None, None, :]
    )
    qkv_rows = project(normalize(stream), win_qkv).astype(jnp.bfloat16)
    attended = jax.vmap(plain_windows)(qkv_rows)
    stream = stream + project(attended, win_out)
    stream = feed_forward(stream, win_up, win_down)
    groups = lax.axis_size("member")
    amount = height * breadth // groups
    normed = normalize(stream).reshape(members, groups, amount, channels)
    mixed = member_attention(
        project(
            lax.all_to_all(normed, "member", split_axis=1, concat_axis=0, tiled=True), mem_qkv
        ).astype(jnp.bfloat16)
    )
    returned = lax.all_to_all(mixed, "member", split_axis=0, concat_axis=1, tiled=True)
    stream = stream + project(returned.reshape(members, height, breadth, channels), mem_out)
    normed_late = normalize(stream)
    rim = with_halo(normed_late, (("lat", 1), ("lon", 2)), WIN - 1)
    borders = project(rim, shift_qkv[:, channels:]).astype(jnp.bfloat16)
    queries = project(normed_late, shift_qkv[:, :channels]).astype(jnp.bfloat16)
    lat_first = lax.axis_index("lat") * height
    lon_first = lax.axis_index("lon") * breadth
    attended = shifted_attention(
        queries,
        borders,
        offsets,
        lat_first,
        lon_first,
        height * lax.axis_size("lat"),
        breadth * lax.axis_size("lon"),
    )
    stream = stream + project(attended, shift_out)
    stream = feed_forward(stream, shift_up, shift_down)
    return stream.astype(jnp.bfloat16)


def solution(mesh):
    return jax.shard_map(
        per_device,
        mesh=mesh,
        in_specs=(
            P("member", "lat", "lon", None),
            P("lat", "lon"),
            P(),
            P(),
            P(),
            P(),
            P(),
            P(),
            P(),
            P(),
            P(),
            P(),
            P(),
            P(),
        ),
        out_specs=P("member", "lat", "lon", None),
        check_vma=False,
    )
```

profile of v0, /device:TPU:1, one launch (start us, length us, event | category | flops | bytes accessed | tf_op | source)
XLA Modules:
  0.0 118.3 jit_solution(4198648451573722139)
XLA Ops:
  10.2 4.1 %fusion.194 = (f32[3,16,8]{2,1,0:T(8,128)S(1)}, f32[3,16,8,256]{3,2,1,0:T(8,128)S(1)}) fusion(f32[3,16,8,256]{3,2,1,0:T(8,128)S(1)} %get-tuple-element.110, bf16[1024,256]{1,0:T(8,128)(2,1)S(1)} %copy-done.10, f32[3,16,8,1024]{3,2,1,0:T(8,128)S(1)} %get-tuple-element.111, u16[3,8,1024]{2,1,0:T(8,128)(2,1)S(1)} %get-tuple-element.80, ...), kind=kOutput, calls=%fused_computation.267 | convolution fusion | flops 229047936 | bytes 2983424 | tf_op jit(solution)/shard_map/dot_general | solution.py:36
  15.4 10.2 %all-to-all-start = ((bf16[3,4,32,256]{3,2,0,1:T(8,128)(2,1)}), bf16[3,4,32,256]{3,2,0,1:T(8,128)(2,1)S(1)}, u32[]{:S(2)}, u32[]{:S(2)}) async-start(bf16[3,4,32,256]{3,2,0,1:T(8,128)(2,1)} %copy.56), calls=%async_computation | async-start | bytes 393216 | tf_op jit(solution)/shard_map/all_to_all | solution.py:164
  27.6 3.6 %all-to-all-done = bf16[3,4,32,256]{3,2,0,1:T(8,128)(2,1)S(1)} async-done(((bf16[3,4,32,256]{3,2,0,1:T(8,128)(2,1)}), bf16[3,4,32,256]{3,2,0,1:T(8,128)(2,1)S(1)}, u32[]{:S(2)}, u32[]{:S(2)}) %all-to-all-start) | async-done | bytes 196640 | tf_op jit(solution)/shard_map/all_to_all | solution.py:164
  35.3 4.6 %all-to-all-start.1 = ((bf16[12,1,32,256]{3,2,1,0:T(8,128)(2,1)}), bf16[12,1,32,256]{3,2,1,0:T(8,128)(2,1)S(1)}, u32[]{:S(2)}, u32[]{:S(2)}) async-start(bf16[12,1,32,256]{3,2,1,0:T(8,128)(2,1)} %bitcast.22), calls=%async_computation.1 | async-start | bytes 393216 | tf_op jit(solution)/shard_map/all_to_all | solution.py:167
  40.5 4.9 %all-to-all-done.1 = bf16[12,1,32,256]{3,2,1,0:T(8,128)(2,1)S(1)} async-done(((bf16[12,1,32,256]{3,2,1,0:T(8,128)(2,1)}), bf16[12,1,32,256]{3,2,1,0:T(8,128)(2,1)S(1)}, u32[]{:S(2)}, u32[]{:S(2)}) %all-to-all-start.1) | async-done | bytes 196640 | tf_op jit(solution)/shard_map/all_to_all | solution.py:167
  46.3 1.9 %collective-permute-start = (bf16[3,7,8,256]{3,2,1,0:T(8,128)(2,1)S(1)}, bf16[3,7,8,256]{3,2,1,0:T(8,128)(2,1)S(1)}, u32[]{:S(2)}, u32[]{:S(2)}) collective-permute-start(bf16[3,7,8,256]{3,2,1,0:T(8,128)(2,1)S(1)} %get-tuple-element.105), channel_id=1, source_target_pairs={{0,16},{16,32},{32,48},{48,64},{64,80},{80,96},{96,112},{112,0},{1... | collective-permute-start | bytes 258056 | tf_op jit(solution)/shard_map/ppermute | solution.py:19
  48.2 5.5 %collective-permute-start.1 = (bf16[3,7,8,256]{3,2,1,0:T(8,128)(2,1)S(1)}, bf16[3,7,8,256]{3,2,1,0:T(8,128)(2,1)S(1)}, u32[]{:S(2)}, u32[]{:S(2)}) collective-permute-start(bf16[3,7,8,256]{3,2,1,0:T(8,128)(2,1)S(1)} %get-tuple-element.106), channel_id=1, source_target_pairs={{16,0},{32,16},{48,32},{64,48},{80,64},{96,80},{112,96},{0,112},{1... | collective-permute-start | bytes 258056 | tf_op jit(solution)/shard_map/ppermute | solution.py:22
  56.6 1.9 %collective-permute-start.2 = (bf16[3,30,7,256]{3,2,1,0:T(8,128)(2,1)}, bf16[3,30,7,256]{3,2,1,0:T(8,128)(2,1)S(1)}, u32[]{:S(2)}, u32[]{:S(2)}) collective-permute-start(bf16[3,30,7,256]{3,2,1,0:T(8,128)(2,1)} %get-tuple-element.103), channel_id=1, source_target_pairs={{0,1},{1,2},{2,3},{3,4},{4,5},{5,6},{6,7},{7,8},{8,9},{9,10},{10,1... | collective-permute-start | bytes 967688 | tf_op jit(solution)/shard_map/ppermute | solution.py:19
  58.5 7.2 %collective-permute-start.3 = (bf16[3,30,7,256]{3,2,1,0:T(8,128)(2,1)S(1)}, bf16[3,30,7,256]{3,2,1,0:T(8,128)(2,1)S(1)}, u32[]{:S(2)}, u32[]{:S(2)}) collective-permute-start(bf16[3,30,7,256]{3,2,1,0:T(8,128)(2,1)S(1)} %get-tuple-element.104), channel_id=1, source_target_pairs={{1,0},{2,1},{3,2},{4,3},{5,4},{6,5},{7,6},{8,7},{9,8},{10,9},{11,1... | collective-permute-start | bytes 967688 | tf_op jit(solution)/shard_map/ppermute | solution.py:22
  67.1 3.9 %collective-permute-done.2 = bf16[3,30,7,256]{3,2,1,0:T(8,128)(2,1)S(1)} collective-permute-done((bf16[3,30,7,256]{3,2,1,0:T(8,128)(2,1)}, bf16[3,30,7,256]{3,2,1,0:T(8,128)(2,1)S(1)}, u32[]{:S(2)}, u32[]{:S(2)}) %collective-permute-start.2) | collective-permute-done | bytes 322592 | tf_op jit(solution)/shard_map/ppermute | solution.py:19
  75.8 3.3 %reshape.363 = bf16[3,660,4,64]{3,2,1,0:T(4,128)(2,1)S(1)} reshape(bf16[3,30,22,256]{3,2,1,0:T(8,128)(2,1)} %copy.65) | data formatting | bytes 2027520 | tf_op jit(solution)/shard_map/reshape | solution.py:117
  79.1 3.7 %copy.67 = bf16[3,660,4,64]{1,3,2,0:T(8,128)(2,1)} copy(bf16[3,660,4,64]{3,2,1,0:T(4,128)(2,1)S(1)} %reshape.363) | data formatting | bytes 2027520
  82.9 2.8 %copy.66 = bf16[3,30,22,256]{3,2,1,0:T(8,128)(2,1)} copy(bf16[3,30,22,256]{3,1,2,0:T(8,128)(2,1)} %get-tuple-element.95) | data formatting | bytes 2027520 | tf_op jit(solution)/shard_map/slice | solution.py:116
  85.7 3.3 %reshape.365 = bf16[3,660,4,64]{3,2,1,0:T(4,128)(2,1)S(1)} reshape(bf16[3,30,22,256]{3,2,1,0:T(8,128)(2,1)} %copy.66) | data formatting | bytes 2027520 | tf_op jit(solution)/shard_map/reshape | solution.py:116
  89.0 3.8 %copy.69 = bf16[3,660,4,64]{1,3,2,0:T(8,128)(2,1)} copy(bf16[3,660,4,64]{3,2,1,0:T(4,128)(2,1)S(1)} %reshape.365) | data formatting | bytes 2027520
  92.8 18.9 %while.11 = (s32[]{:T(128)}, bf16[3,128,4,64]{1,3,2,0:T(8,128)(2,1)S(1)}, bf16[3,660,4,64]{1,3,2,0:T(8,128)(2,1)}, bf16[3,128,4,64]{1,3,2,0:T(8,128)(2,1)S(1)}, ...) while((s32[]{:T(128)}, ...), condition=%wide.region_15.16_spmd.clone, body=%wide.region_12.15_spmd.clone.sunk | while | flops 132921632 | bytes 1976549 | solution.py:130
  93.2 1.8 %broadcast_in_dim.85 = pred[128,660]{1,0:T(8,128)(4,1)S(1)} reshape(pred[16,8,30,22]{3,2,1,0:T(8,128)(4,1)S(1)} %broadcast_and_fusion.2) | data formatting | bytes 168960 | tf_op jit(solution)/shard_map/while/body/eval_jaxpr/jit(_where)/broadcast_in_dim | solution.py:124
  95.2 1.9 %fusion.216 = f32[4,128]{1,0:T(4,128)S(1)} fusion(pred[128,660]{0,1:T(8,128)(4,1)S(1)} %copy.122, bf16[3,660,4,64]{1,3,2,0:T(8,128)(2,1)} %get-tuple-element.184, s32[]{:T(128)} %get-tuple-element.172, bf16[3,128,4,64]{1,3,2,0:T(8,128)(2,1)S(1)} %get-tuple-element.183), kind=kOutput, calls=%fused_computation.258.clone.1 | convolution fusion | flops 44606100 | bytes 546816 | tf_op jit(solution)/shard_map/while/body/eval_jaxpr/sub | solution.py:125
  97.0 2.1 %fusion.217 = bf16[3,128,4,64]{1,3,2,0:T(8,128)(2,1)S(1)} fusion(bf16[3,128,4,64]{1,3,2,0:T(8,128)(2,1)S(1)} %get-tuple-element.173, s32[]{:T(128)} %get-tuple-element.172, f32[4,128]{1,0:T(4,128)S(1)} %fusion.216, bf16[3,660,4,64]{1,3,2,0:T(8,128)(2,1)} %get-tuple-element.182, pred[128,660]{0,1:T(8,128)(4,1)S(1)} %copy.122, ...), kind=kOutput, calls=%fused_computation.9.clone.1 | convolution fusion | flops 88231056 | bytes 1006592 | tf_op jit(solution)/shard_map/while/body/eval_jaxpr/hqk,khe->qhe/dot_general | solution.py:126
  101.5 1.8 %fusion.216 = f32[4,128]{1,0:T(4,128)S(1)} fusion(pred[128,660]{0,1:T(8,128)(4,1)S(1)} %copy.122, bf16[3,660,4,64]{1,3,2,0:T(8,128)(2,1)} %get-tuple-element.184, s32[]{:T(128)} %get-tuple-element.172, bf16[3,128,4,64]{1,3,2,0:T(8,128)(2,1)S(1)} %get-tuple-element.183), kind=kOutput, calls=%fused_computation.258.clone.1 | convolution fusion | flops 44606100 | bytes 546816 | tf_op jit(solution)/shard_map/while/body/eval_jaxpr/sub | solution.py:125
  103.3 2.1 %fusion.217 = bf16[3,128,4,64]{1,3,2,0:T(8,128)(2,1)S(1)} fusion(bf16[3,128,4,64]{1,3,2,0:T(8,128)(2,1)S(1)} %get-tuple-element.173, s32[]{:T(128)} %get-tuple-element.172, f32[4,128]{1,0:T(4,128)S(1)} %fusion.216, bf16[3,660,4,64]{1,3,2,0:T(8,128)(2,1)} %get-tuple-element.182, pred[128,660]{0,1:T(8,128)(4,1)S(1)} %copy.122, ...), kind=kOutput, calls=%fused_computation.9.clone.1 | convolution fusion | flops 88231056 | bytes 1006592 | tf_op jit(solution)/shard_map/while/body/eval_jaxpr/hqk,khe->qhe/dot_general | solution.py:126
  107.8 1.8 %fusion.216 = f32[4,128]{1,0:T(4,128)S(1)} fusion(pred[128,660]{0,1:T(8,128)(4,1)S(1)} %copy.122, bf16[3,660,4,64]{1,3,2,0:T(8,128)(2,1)} %get-tuple-element.184, s32[]{:T(128)} %get-tuple-element.172, bf16[3,128,4,64]{1,3,2,0:T(8,128)(2,1)S(1)} %get-tuple-element.183), kind=kOutput, calls=%fused_computation.258.clone.1 | convolution fusion | flops 44606100 | bytes 546816 | tf_op jit(solution)/shard_map/while/body/eval_jaxpr/sub | solution.py:125
  109.6 2.1 %fusion.217 = bf16[3,128,4,64]{1,3,2,0:T(8,128)(2,1)S(1)} fusion(bf16[3,128,4,64]{1,3,2,0:T(8,128)(2,1)S(1)} %get-tuple-element.173, s32[]{:T(128)} %get-tuple-element.172, f32[4,128]{1,0:T(4,128)S(1)} %fusion.216, bf16[3,660,4,64]{1,3,2,0:T(8,128)(2,1)} %get-tuple-element.182, pred[128,660]{0,1:T(8,128)(4,1)S(1)} %copy.122, ...), kind=kOutput, calls=%fused_computation.9.clone.1 | convolution fusion | flops 88231056 | bytes 1006592 | tf_op jit(solution)/shard_map/while/body/eval_jaxpr/hqk,khe->qhe/dot_general | solution.py:126
  114.0 4.4 %fusion.72 = bf16[3,16,8,256]{3,2,1,0:T(8,128)(2,1)} fusion(f32[3,16,8,256]{3,2,1,0:T(8,128)S(1)} %get-tuple-element.119, f32[3,16,8,1024]{3,2,1,0:T(8,128)S(1)} %get-tuple-element.120, bf16[1024,256]{1,0:T(8,128)(2,1)S(1)} %copy-done.12, u16[3,8,1024]{2,1,0:T(8,128)(2,1)S(1)} %get-tuple-element.78, u16[3,8,1024]{2,1,0:T(8,128)(2,1)S(1)} %get-tuple-element.77), kind=kOutput, calls=%fused_computation.91 | convolution fusion | flops 229048320 | bytes 2785280 | tf_op jit(solution)/shard_map/dot_general | solution.py:36
  (101 shorter events, 34.9 us)
Async XLA Ops:
  0.0 9.1 %copy-start = (bf16[256,1024]{1,0:T(8,128)(2,1)S(1)}, bf16[256,1024]{1,0:T(8,128)(2,1)}, u32[]{:S(2)}) copy-start(bf16[256,1024]{1,0:T(8,128)(2,1)} %param.22) | copy-start | bytes 1572868
  7.6 0.9 copy-start.1
  7.6 1.0 copy-start.8
  9.2 1.0 copy-start.10
  14.3 11.3 %copy-start.9 = (s32[2]{0:T(128)S(1)}, s32[2]{0:T(128)}, u32[]{:S(2)}) copy-start(s32[2]{0:T(128)} %param.18) | copy-start | bytes 28
  14.3 16.9 %copy-start.2 = (bf16[256,768]{1,0:T(8,128)(2,1)S(1)}, bf16[256,768]{1,0:T(8,128)(2,1)}, u32[]{:S(2)}) copy-start(bf16[256,768]{1,0:T(8,128)(2,1)} %param.24) | copy-start | bytes 1179652
  15.4 15.8 %all-to-all-start = ((bf16[3,4,32,256]{3,2,0,1:T(8,128)(2,1)}), bf16[3,4,32,256]{3,2,0,1:T(8,128)(2,1)S(1)}, u32[]{:S(2)}, u32[]{:S(2)}) async-start(bf16[3,4,32,256]{3,2,0,1:T(8,128)(2,1)} %copy.56), calls=%async_computation | async-start | bytes 393216 | tf_op jit(solution)/shard_map/all_to_all | solution.py:164
  34.2 11.3 %copy-start.6 = (bf16[256,256]{1,0:T(8,128)(2,1)S(1)}, bf16[256,256]{1,0:T(8,128)(2,1)}, u32[]{:S(2)}) copy-start(bf16[256,256]{1,0:T(8,128)(2,1)} %param.25) | copy-start | bytes 393220
  35.3 10.1 %all-to-all-start.1 = ((bf16[12,1,32,256]{3,2,1,0:T(8,128)(2,1)}), bf16[12,1,32,256]{3,2,1,0:T(8,128)(2,1)S(1)}, u32[]{:S(2)}, u32[]{:S(2)}) async-start(bf16[12,1,32,256]{3,2,1,0:T(8,128)(2,1)} %bitcast.22), calls=%async_computation.1 | async-start | bytes 393216 | tf_op jit(solution)/shard_map/all_to_all | solution.py:167
  46.1 19.7 %copy-start.3 = (bf16[256,768]{1,0:T(8,128)(2,1)S(1)}, bf16[256,768]{1,0:T(8,128)(2,1)}, u32[]{:S(2)}) copy-start(bf16[256,768]{1,0:T(8,128)(2,1)} %param.26) | copy-start | bytes 1179652
  46.3 8.0 %collective-permute-start = (bf16[3,7,8,256]{3,2,1,0:T(8,128)(2,1)S(1)}, bf16[3,7,8,256]{3,2,1,0:T(8,128)(2,1)S(1)}, u32[]{:S(2)}, u32[]{:S(2)}) collective-permute-start(bf16[3,7,8,256]{3,2,1,0:T(8,128)(2,1)S(1)} %get-tuple-element.105), channel_id=1, source_target_pairs={{0,16},{16,32},{32,48},{48,64},{64,80},{80,96},{96,112},{112,0},{1... | collective-permute-start | bytes 258056 | tf_op jit(solution)/shard_map/ppermute | solution.py:19
  48.2 7.5 %collective-permute-start.1 = (bf16[3,7,8,256]{3,2,1,0:T(8,128)(2,1)S(1)}, bf16[3,7,8,256]{3,2,1,0:T(8,128)(2,1)S(1)}, u32[]{:S(2)}, u32[]{:S(2)}) collective-permute-start(bf16[3,7,8,256]{3,2,1,0:T(8,128)(2,1)S(1)} %get-tuple-element.106), channel_id=1, source_target_pairs={{16,0},{32,16},{48,32},{64,48},{80,64},{96,80},{112,96},{0,112},{1... | collective-permute-start | bytes 258056 | tf_op jit(solution)/shard_map/ppermute | solution.py:22
  56.6 14.4 %collective-permute-start.2 = (bf16[3,30,7,256]{3,2,1,0:T(8,128)(2,1)}, bf16[3,30,7,256]{3,2,1,0:T(8,128)(2,1)S(1)}, u32[]{:S(2)}, u32[]{:S(2)}) collective-permute-start(bf16[3,30,7,256]{3,2,1,0:T(8,128)(2,1)} %get-tuple-element.103), channel_id=1, source_target_pairs={{0,1},{1,2},{2,3},{3,4},{4,5},{5,6},{6,7},{7,8},{8,9},{9,10},{10,1... | collective-permute-start | bytes 967688 | tf_op jit(solution)/shard_map/ppermute | solution.py:19
  58.5 13.2 %collective-permute-start.3 = (bf16[3,30,7,256]{3,2,1,0:T(8,128)(2,1)S(1)}, bf16[3,30,7,256]{3,2,1,0:T(8,128)(2,1)S(1)}, u32[]{:S(2)}, u32[]{:S(2)}) collective-permute-start(bf16[3,30,7,256]{3,2,1,0:T(8,128)(2,1)S(1)} %get-tuple-element.104), channel_id=1, source_target_pairs={{1,0},{2,1},{3,2},{4,3},{5,4},{6,5},{7,6},{8,7},{9,8},{10,9},{11,1... | collective-permute-start | bytes 967688 | tf_op jit(solution)/shard_map/ppermute | solution.py:22
  89.0 3.8 %copy-start.4 = (bf16[3,128,4,64]{1,3,2,0:T(8,128)(2,1)S(1)}, bf16[3,128,4,64]{1,3,2,0:T(8,128)(2,1)}, u32[]{:S(2)}) copy-start(bf16[3,128,4,64]{1,3,2,0:T(8,128)(2,1)} %copy.68) | copy-start | bytes 589828
  89.0 3.8 %copy-start.5 = (bf16[3,128,4,64]{1,3,2,0:T(8,128)(2,1)S(1)}, bf16[3,128,4,64]{1,3,2,0:T(8,128)(2,1)}, u32[]{:S(2)}) copy-start(bf16[3,128,4,64]{1,3,2,0:T(8,128)(2,1)} %custom-call) | copy-start | bytes 589828
  92.8 19.5 %copy-start.7 = (bf16[256,256]{1,0:T(8,128)(2,1)S(1)}, bf16[256,256]{1,0:T(8,128)(2,1)}, u32[]{:S(2)}) copy-start(bf16[256,256]{1,0:T(8,128)(2,1)} %param.27) | copy-start | bytes 393220
  111.8 1.1 copy-start.11
  112.9 1.0 copy-start.12
where the time goes:
time: 120 us; the launch traced here: 118 us
  local copies, waits for them, and re-layouts  34.7 us (29%)
  starting transfers between devices  31.2 us (26%)
  matrix products  27.9 us (23%)
  waiting for transfers between devices  14.6 us (12%)
  other arithmetic  9.28 us (8%)
    dot_general x11, matrix products, project(): result = jnp.dot(flattened, matrix, preferred_element_type=jnp.float32)  13.5 us
    ppermute x2, starting transfers between devices, with_halo(): lax.ppermute(lax.slice_in_dim(block, 0, width, axis=dim), axis, backward)  12.6 us
    all_to_all x1, starting transfers between devices, per_device(): lax.all_to_all(normed, 'member', split_axis=1, concat_axis=0, tiled=True)  10.2 us
    unnamed x30, local copies, waits for them, and re-layouts  9.44 us
    dot_general x3, matrix products, attend_member(): jnp.einsum('hqk,khe->qhe', weights, value_part, preferred_element_type=jn...  6.37 us
    broadcast_in_dim x6, local copies, waits for them, and re-layouts, attend_member(): scores = jnp.where(allowed[None], scores, -1e+30)  6.02 us
    sub x3, matrix products, attend_member(): weights = jax.nn.softmax(scores, axis=-1).astype(jnp.bfloat16)  5.55 us
    all_to_all x1, waiting for transfers between devices, per_device(): lax.all_to_all(mixed, 'member', split_axis=0, concat_axis=1, tiled=True)  4.94 us
  transfers between devices with their start and end apart: 6, of which 5 were waited for; matrix products, arithmetic and copies ran while one was open for 4% of the time, Pallas kernels for 0%

commit v1 on v0

v1 whole, which is shorter than its diff:
```python
import functools

import jax
import jax.numpy as jnp
from jax import lax
from jax.experimental import pallas as pl
from jax.experimental.pallas import tpu as pltpu
from jax.sharding import PartitionSpec as P

HEADS = 4
WIN = 8
EPS = 1e-05
NEG = -1e30
MESH = pl.DeviceIdType.MESH
BF = jnp.bfloat16
F32 = jnp.float32


def normalize(stream):
    average = jnp.mean(stream, axis=-1, keepdims=True)
    centered = stream - average
    spread = jnp.mean(centered * centered, axis=-1, keepdims=True)
    return (centered * lax.rsqrt(spread + EPS)).astype(BF)


def project(inputs, matrix):
    return jnp.dot(inputs, matrix, preferred_element_type=F32)


def gelu(x):
    return (0.5 * x) * (1.0 + lax.erf(x * 0.7071067811865476))


def feed_forward(stream, w_up, w_down):
    hidden = gelu(project(normalize(stream), w_up)).astype(BF)
    return stream + project(hidden, w_down)


def head_masks(channels, dtype):
    lane = lax.broadcasted_iota(jnp.int32, (1, channels), 1) // (channels // HEADS)
    return [jnp.where(lane == h, 1.0, 0.0).astype(dtype) for h in range(HEADS)]


def attend(q, k, v, bias, masks_bf, masks_f32):
    count = q.shape[0]
    stacked = jnp.concatenate([q * mask for mask in masks_bf], axis=0)
    scores = lax.dot_general(
        stacked, k, (((1,), (1,)), ((), ())), preferred_element_type=F32
    )
    if bias is not None:
        scores = (
            scores.reshape(HEADS, count, -1) + bias[None]
        ).reshape(scores.shape)
    top = jnp.max(scores, axis=-1, keepdims=True)
    weights = jnp.exp(scores - top)
    total = jnp.sum(weights, axis=-1, keepdims=True)
    weights = (weights * (1.0 / total)).astype(BF)
    wide = project(weights, v)
    result = wide[:count] * masks_f32[0]
    for h in range(1, HEADS):
        result = result + wide[h * count : (h + 1) * count] * masks_f32[h]
    return result


def kernel(
    sizes,
    fields, land, offsets, embed,
    h_win_qkv, h_win_out, h_win_up, h_win_down, h_mem_qkv, h_mem_out,
    h_shift_qkv, h_shift_out, h_shift_up, h_shift_down,
    out,
    win_qkv, win_out, win_up, win_down, mem_qkv, mem_out,
    shift_qkv, shift_out, shift_up, shift_down,
    stream, mine, got, qkv, mixed, mixed_send, mixed_got,
    late, vert, left, right, corner, corner_left, corner_right,
    biases,
    w_sem, a_send, a_recv, r_send, r_recv, v_send, v_recv,
    l_send, l_recv, rt_send, rt_recv, c_send, c_recv,
):
    n_member, n_lat, n_lon = sizes
    members = fields.shape[0]
    channels = fields.shape[-1]
    tokens = WIN * WIN
    me = lax.axis_index("member")
    lat = lax.axis_index("lat")
    lon = lax.axis_index("lon")
    core = lax.rem(me, 2)
    chip = me // 2
    other = 1 - core
    mate = {"member": 2 * chip + other}
    far_same = {"member": 2 * (1 - chip) + core}
    far_other = {"member": 2 * (1 - chip) + other}
    lat_up = {"lat": lax.rem(lat + n_lat - 1, n_lat)}
    lat_down = {"lat": lax.rem(lat + 1, n_lat)}
    lon_left = {"lon": lax.rem(lon + n_lon - 1, n_lon)}
    lon_right = {"lon": lax.rem(lon + 1, n_lon)}

    barrier = pltpu.get_barrier_semaphore()
    for peer in (mate, far_same, far_other, lat_up, lat_down, lon_left, lon_right):
        pl.semaphore_signal(barrier, inc=1, device_id=peer, device_id_type=MESH)

    pairs = [
        (h_win_qkv, win_qkv), (h_win_out, win_out), (h_win_up, win_up),
        (h_win_down, win_down), (h_mem_qkv, mem_qkv), (h_mem_out, mem_out),
        (h_shift_qkv, shift_qkv), (h_shift_out, shift_out),
        (h_shift_up, shift_up), (h_shift_down, shift_down),
    ]
    loads = [
        pltpu.make_async_copy(source, target, w_sem.at[i])
        for i, (source, target) in enumerate(pairs)
    ]
    for load in loads:
        load.start()

    off0 = offsets[0]
    off1 = offsets[1]
    split0 = WIN - off0
    split1 = WIN - off1
    masks_bf = head_masks(channels, BF)
    masks_f32 = head_masks(channels, F32)
    scale = (channels // HEADS) ** -0.5

    def push(source, target, send, recv, peer):
        copy = pltpu.make_async_remote_copy(
            src_ref=source, dst_ref=target, send_sem=send, recv_sem=recv,
            device_id=peer, device_id_type=MESH,
        )
        copy.start()
        return copy

    token = lax.broadcasted_iota(jnp.int32, (tokens, channels), 0)
    row_low = jnp.where(token // WIN < split0, 1.0, 0.0)
    col_low = jnp.where(lax.rem(token, WIN) < split1, 1.0, 0.0)
    mr, nr = row_low.astype(BF), (1.0 - row_low).astype(BF)
    mc, nc = col_low.astype(BF), (1.0 - col_low).astype(BF)
    q_tok = lax.broadcasted_iota(jnp.int32, (tokens, 4 * tokens), 0)
    k_tok = lax.broadcasted_iota(jnp.int32, (tokens, 4 * tokens), 1)
    q_row = jnp.where(q_tok // WIN < split0, 1, 0)
    q_col = jnp.where(lax.rem(q_tok, WIN) < split1, 1, 0)
    k_row = k_tok // (2 * tokens)
    k_col = lax.rem(k_tok // tokens, 2)
    k_low = jnp.where(lax.rem(k_tok, tokens) // WIN < split0, 1, 0)
    wrong = jnp.where(q_row == k_row, 0.0, NEG) + jnp.where(q_col == k_col, 0.0, NEG)
    first = jnp.where(lat == 0, 1.0, 0.0)
    last = jnp.where(lat == n_lat - 1, 1.0, 0.0)
    outside0 = jnp.where(k_row == 0, jnp.where(k_low == 1, NEG, 0.0), 0.0) * first
    outside1 = jnp.where(k_row == 1, jnp.where(k_low == 0, NEG, 0.0), 0.0) * last
    biases[0] = wrong + outside0
    biases[1] = wrong + outside1

    def window_block(block):
        s_row = lax.broadcasted_iota(jnp.int32, (tokens, WIN), 0)
        s_lane = lax.broadcasted_iota(jnp.int32, (tokens, WIN), 1)
        rows = [WIN * block + lax.rem(s + off0, WIN) for s in range(WIN)]
        spread = jnp.concatenate(
            [jnp.broadcast_to(land[pl.ds(r, 1), :], (WIN, WIN)) for r in rows], axis=0
        )
        picked = jnp.where(
            s_lane == lax.rem(lax.rem(s_row, WIN) + off1, WIN), spread.astype(F32), 0.0
        )
        is_land = jnp.sum(picked, axis=-1, keepdims=True)
        added = is_land * embed[...]
        parts = []
        for m in range(members):
            tile = jnp.concatenate(
                [fields[m, r].astype(F32).reshape(1, WIN, channels) for r in rows], axis=0
            )
            tile = pltpu.roll(tile, split1, 1)
            parts.append(tile.reshape(tokens, channels) + added)
        x = jnp.concatenate(parts, axis=0)
        return x

    def window_section(block, waits):
        x = window_block(block)
        if waits:
            loads[0].wait()
        proj = project(normalize(x), win_qkv[...])
        atts = []
        for m in range(members):
            rows = slice(m * tokens, (m + 1) * tokens)
            q = (proj[rows, :channels] * scale).astype(BF)
            k = proj[rows, channels : 2 * channels].astype(BF)
            v = proj[rows, 2 * channels :].astype(BF)
            atts.append(attend(q, k, v, None, masks_bf, masks_f32))
        if waits:
            loads[1].wait()
        x = x + project(jnp.concatenate(atts, axis=0).astype(BF), win_out[...])
        if waits:
            loads[2].wait()
            loads[3].wait()
        x = feed_forward(x, win_up[...], win_down[...])
        stream[block] = x.reshape(members, WIN, WIN, channels)
        mine[block] = normalize(x).reshape(members, tokens, channels)

    window_section(other, True)
    pl.semaphore_wait(barrier, 7)
    sends = [
        push(mine.at[other], got.at[2], a_send.at[2], a_recv.at[2], far_other),
        push(mine.at[other], got.at[0], a_send.at[0], a_recv.at[0], mate),
    ]
    window_section(core, False)
    sends.append(push(mine.at[core], got.at[1], a_send.at[1], a_recv.at[1], far_same))

    loads[4].wait()

    def member_qkv(source, x, with_q):
        weights = mem_qkv[...] if with_q else mem_qkv[:, channels:]
        first_col = 0 if with_q else channels
        qkv[source, :, :, first_col:] = project(
            x.reshape(members * tokens, channels), weights
        ).reshape(members, tokens, -1)

    member_qkv(0, mine[core], True)
    sends[1].wait_recv()
    member_qkv(1, got[0], True)
    sends[0].wait_recv()
    member_qkv(2, got[2], False)
    sends[2].wait_recv()
    member_qkv(3, got[1], False)

    near = 2 * members
    total = 4 * members
    qt = lax.rem(lax.broadcasted_iota(jnp.int32, (near * WIN, total * WIN), 0), WIN)
    kt = lax.rem(lax.broadcasted_iota(jnp.int32, (near * WIN, total * WIN), 1), WIN)
    same_token = jnp.where(qt == kt, 0.0, NEG)
    for group in range(tokens // WIN):
        span = slice(group * WIN, (group + 1) * WIN)
        q = qkv[0:2, :, span, 0:channels].reshape(near * WIN, channels)
        k = qkv[:, :, span, channels : 2 * channels].reshape(total * WIN, channels)
        v = qkv[:, :, span, 2 * channels :].reshape(total * WIN, channels)
        att = attend(
            (q * scale).astype(BF), k.astype(BF), v.astype(BF), same_token,
            masks_bf, masks_f32,
        )
        mixed[:, :, span, :] = att.reshape(2, members, WIN, channels)
    mixed_send[...] = mixed[1].astype(BF)
    back = push(mixed_send, mixed_got, r_send, r_recv, mate)
    loads[5].wait()

    def member_add(block, att):
        x = stream[block].reshape(members * tokens, channels)
        x = x + project(att, mem_out[...])
        stream[block] = x.reshape(members, WIN, WIN, channels)
        late[block] = normalize(x).reshape(members, tokens, channels)

    halo = []

    def send_halo(block):
        toward = {"lat": lax.rem(lat + 2 * block - 1 + n_lat, n_lat)}
        for m in range(members):
            piece = late.at[block, m]
            halo.append(
                push(piece, vert.at[1 - block, m], v_send.at[block, m],
                     v_recv.at[1 - block, m], toward)
            )
            halo.append(
                push(piece, right.at[block, m], l_send.at[block, m],
                     l_recv.at[block, m], lon_left)
            )
            halo.append(
                push(piece, left.at[block, m], rt_send.at[block, m],
                     rt_recv.at[block, m], lon_right)
            )

    member_add(core, mixed[0].reshape(members * tokens, channels).astype(BF))
    send_halo(core)
    back.wait_recv()
    member_add(other, mixed_got[...].reshape(members * tokens, channels))
    send_halo(other)

    def arrived(buffer, sem):
        pltpu.make_async_copy(buffer, buffer, sem).wait()

    corners = []
    for m in range(members):
        arrived(vert.at[0, m], v_recv.at[0, m])
        arrived(vert.at[1, m], v_recv.at[1, m])
        corner[m] = vert[0, m] * mr + vert[1, m] * nr
        corners.append(
            push(corner.at[m], corner_right.at[m], c_send.at[0, m], c_recv.at[0, m], lon_left)
        )
        corners.append(
            push(corner.at[m], corner_left.at[m], c_send.at[1, m], c_recv.at[1, m], lon_right)
        )

    for load in loads[6:]:
        load.wait()

    for m in range(members):
        for block in range(2):
            arrived(right.at[block, m], l_recv.at[block, m])
            arrived(left.at[block, m], rt_recv.at[block, m])
        arrived(corner_right.at[m], c_recv.at[0, m])
        arrived(corner_left.at[m], c_recv.at[1, m])
        own = [late[0, m], late[1, m]]
        edge = corner[m]
        side = [left[b, m] * mc + right[b, m] * nc for b in range(2)]
        far = corner_left[m] * mc + corner_right[m] * nc
        middle = [edge * mr + own[0] * nr, own[0] * mr + own[1] * nr, own[1] * mr + edge * nr]
        flank = [far * mr + side[0] * nr, side[0] * mr + side[1] * nr, side[1] * mr + far * nr]
        windows = []
        for g in range(3):
            windows.append(flank[g] * mc + middle[g] * nc)
            windows.append(middle[g] * mc + flank[g] * nc)
        keyed = project(jnp.concatenate(windows, axis=0), shift_qkv[:, channels:]).astype(BF)
        asked = project(jnp.concatenate(own, axis=0), shift_qkv[:, :channels])
        asked = (asked * scale).astype(BF)
        atts = []
        for b in range(2):
            keys = slice(2 * tokens * b, 2 * tokens * b + 4 * tokens)
            atts.append(
                attend(
                    asked[b * tokens : (b + 1) * tokens], keyed[keys, :channels],
                    keyed[keys, channels:], biases[b], masks_bf, masks_f32,
                )
            )
        x = jnp.concatenate(
            [stream[b, m].reshape(tokens, channels) for b in range(2)], axis=0
        )
        x = x + project(jnp.concatenate(atts, axis=0).astype(BF), shift_out[...])
        x = feed_forward(x, shift_up[...], shift_down[...])
        for b in range(2):
            stream[b, m] = x[b * tokens : (b + 1) * tokens].reshape(WIN, WIN, channels)
        for b in range(2):
            tile = jnp.concatenate(
                [
                    stream[b, m, lax.rem(r + split0, WIN)].reshape(1, WIN, channels)
                    for r in range(WIN)
                ],
                axis=0,
            )
            tile = pltpu.roll(tile, off1, 1)
            out[m, b * WIN : (b + 1) * WIN] = tile.astype(BF)

    for copy in sends + [back] + halo + corners:
        copy.wait_send()


def per_device(sizes, fields, land_mask, offsets, land_embed, *weights):
    members, height, breadth, channels = fields.shape
    tokens = WIN * WIN
    vmem = pl.BlockSpec(memory_space=pltpu.VMEM)
    tile = (members, tokens, channels)
    dma = pltpu.SemaphoreType.DMA
    scratch = [pltpu.VMEM(w.shape, w.dtype) for w in weights] + [
        pltpu.VMEM((2, members, WIN, WIN, channels), F32),
        pltpu.VMEM((2,) + tile, BF),
        pltpu.VMEM((3,) + tile, BF),
        pltpu.VMEM((4, members, tokens, 3 * channels), F32),
        pltpu.VMEM((2,) + tile, F32),
        pltpu.VMEM(tile, BF),
        pltpu.VMEM(tile, BF),
        pltpu.VMEM((2,) + tile, BF),
        pltpu.VMEM((2,) + tile, BF),
        pltpu.VMEM((2,) + tile, BF),
        pltpu.VMEM((2,) + tile, BF),
        pltpu.VMEM(tile, BF),
        pltpu.VMEM(tile, BF),
        pltpu.VMEM(tile, BF),
        pltpu.VMEM((2, tokens, 4 * tokens), F32),
        dma((len(weights),)),
        dma((3,)), dma((3,)), dma, dma,
        dma((2, members)), dma((2, members)),
        dma((2, members)), dma((2, members)),
        dma((2, members)), dma((2, members)),
        dma((2, members)), dma((2, members)),
    ]
    return pl.pallas_call(
        functools.partial(kernel, sizes),
        out_shape=jax.ShapeDtypeStruct(fields.shape, BF),
        in_specs=[vmem, vmem, pl.BlockSpec(memory_space=pltpu.SMEM), vmem]
        + [pl.BlockSpec(memory_space=pl.ANY)] * len(weights),
        out_specs=vmem,
        scratch_shapes=scratch,
        compiler_params=pltpu.CompilerParams(collective_id=0, has_side_effects=True),
        name="scorer",
    )(fields, land_mask, offsets, land_embed.reshape(1, channels), *weights)


def solution(mesh):
    sizes = tuple(mesh.shape[axis] for axis in ("member", "lat", "lon"))
    return jax.shard_map(
        functools.partial(per_device, sizes),
        mesh=mesh,
        in_specs=(P("member", "lat", "lon", None), P("lat", "lon")) + (P(),) * 12,
        out_specs=P("member", "lat", "lon", None),
        check_vma=False,
    )
```

time: 120 us -> 40.5 us (0.34); the launches traced: 118 us -> 40.3 us
  Pallas kernels: 0 us -> 37.4 us
  local copies, waits for them, and re-layouts: 34.7 us -> 2.97 us
  starting transfers between devices: 31.2 us -> 0 us
  matrix products: 27.9 us -> 0 us
  waiting for transfers between devices: 14.6 us -> 0 us
  other arithmetic: 9.28 us -> 0 us
    pallas_call x0 -> x1, Pallas kernels: none -> 37.4 us  [per_device(): pl.pallas_call(functools.partial(kernel, sizes), out_shape=jax.ShapeDtype...]
    dot_general x17 -> x0, matrix products: 21 us -> none  [the longest x11 13.5 us: project(): result = jnp.dot(flattened, matrix, preferred_element_type=jnp.float32)]
    ppermute x4 -> x0, starting transfers between devices: 16.5 us -> none  [the longest x2 12.6 us: with_halo(): lax.ppermute(lax.slice_in_dim(block, 0, width, axis=dim), axis, backward)]
    all_to_all x2 -> x0, starting transfers between devices: 14.7 us -> none  [the longest x1 10.2 us: per_device(): lax.all_to_all(normed, 'member', split_axis=1, concat_axis=0, tiled=True)]
    reshape x7 -> x0, local copies, waits for them, and re-layouts: 9.74 us -> none  [the longest x1 3.32 us: shifted_attention(): value_heads = borders[..., channels:].reshape(members, -1, HEADS, head_size)]
    all_to_all x2 -> x0, waiting for transfers between devices: 8.53 us -> none  [the longest x1 4.94 us: per_device(): lax.all_to_all(mixed, 'member', split_axis=0, concat_axis=1, tiled=True)]
    slice x8 -> x0, local copies, waits for them, and re-layouts: 8.21 us -> none  [the longest x2 4.02 us: shifted_attention(): key_heads = borders[..., :channels].reshape(members, -1, HEADS, head_size)]
    sub x5 -> x0, matrix products: 6.91 us -> none  [the longest x3 5.55 us: attend_member(): weights = jax.nn.softmax(scores, axis=-1).astype(jnp.bfloat16)]
  transfers between devices with their start and end apart: 6 -> 0, of which waited for: 5 -> 0; matrix products, arithmetic and copies ran while one was open for 4% -> 0% of each run, Pallas kernels for 0% -> 0%
where the time goes in v1:
time: 40.5 us; the launch traced here: 40.3 us
  Pallas kernels  37.4 us (92%)
  local copies, waits for them, and re-layouts  2.97 us (7%)
    pallas_call x1, Pallas kernels, per_device(): pl.pallas_call(functools.partial(kernel, sizes), out_shape=jax.ShapeDtype...  37.4 us
    unnamed x2, local copies, waits for them, and re-layouts  2.97 us

profile of v1, /device:TPU:1, one launch (start us, length us, event | category | flops | bytes accessed | tf_op | source)
XLA Modules:
  0.0 40.3 jit_solution(16988346451576571168)
XLA Ops:
  0.0 1.4 %copy.15.land = s32[16,8]{1,0:T(8,128)} copy(s32[16,8]{0,1:T(8,128)} %param.15) | data formatting | bytes 1024 | tf_op args[1]
  1.4 37.4 %scorer.1 = bf16[3,16,8,256]{3,2,1,0:T(8,128)(2,1)} custom-call(bf16[3,16,8,256]{3,2,1,0:T(8,128)(2,1)} %fields.1, s32[16,8]{1,0:T(8,128)} %copy.15.land, s32[2]{0:T(128)} %offsets.1, f32[1,256]{1,0:T(1,128)} %bitcast.1, bf16[256,768]{1,0:T(8,128)(2,1)} %h_win_qkv.1, bf16[256,256]{1,0:T(8,128)(2,1)} %h_win_out.1, bf16[256,1024]{1,0:T(8,128)(2,1)} %h_win_up.1, ...), custom_call_target="tpu_custom_call" | custom-call | tf_op jit(solution)/shard_map/scorer/pallas_call | solution.py:367
  38.7 1.6 %copy.17 = bf16[3,16,8,256]{3,2,1,0:T(8,128)(2,1)} copy(bf16[3,16,8,256]{3,2,1,0:T(8,128)(2,1)} %scorer.1) | data formatting | bytes 393216

commit v2 on v1

v2 whole, which is shorter than its diff:
```python
import functools

import jax
import jax.numpy as jnp
from jax import lax
from jax.experimental import pallas as pl
from jax.experimental.pallas import tpu as pltpu
from jax.sharding import PartitionSpec as P

HEADS = 4
WIN = 8
EPS = 1e-05
VMEM_LIMIT = 58 * 1024 * 1024
NEG = -1e30
MESH = pl.DeviceIdType.MESH
BF = jnp.bfloat16
F32 = jnp.float32


def normalize(stream):
    average = jnp.mean(stream, axis=-1, keepdims=True)
    centered = stream - average
    spread = jnp.mean(centered * centered, axis=-1, keepdims=True)
    return (centered * lax.rsqrt(spread + EPS)).astype(BF)


def project(inputs, matrix):
    return jnp.dot(inputs, matrix, preferred_element_type=F32)


def gelu(x):
    return (0.5 * x) * (1.0 + lax.erf(x * 0.7071067811865476))


def feed_forward(stream, w_up, w_down):
    hidden = gelu(project(normalize(stream), w_up)).astype(BF)
    return stream + project(hidden, w_down)


def head_masks(channels, dtype):
    lane = lax.broadcasted_iota(jnp.int32, (1, channels), 1) // (channels // HEADS)
    return [jnp.where(lane == h, 1.0, 0.0).astype(dtype) for h in range(HEADS)]


def attend(q, k, v, bias, masks_bf, masks_f32):
    count = q.shape[0]
    stacked = jnp.concatenate([q * mask for mask in masks_bf], axis=0)
    scores = lax.dot_general(
        stacked, k, (((1,), (1,)), ((), ())), preferred_element_type=F32
    )
    if bias is not None:
        scores = (
            scores.reshape(HEADS, count, -1) + bias[None]
        ).reshape(scores.shape)
    top = jnp.max(scores, axis=-1, keepdims=True)
    weights = jnp.exp(scores - top)
    total = jnp.sum(weights, axis=-1, keepdims=True)
    weights = (weights * (1.0 / total)).astype(BF)
    wide = project(weights, v)
    result = wide[:count] * masks_f32[0]
    for h in range(1, HEADS):
        result = result + wide[h * count : (h + 1) * count] * masks_f32[h]
    return result


def kernel(
    sizes,
    h_fields, land, offsets, embed,
    h_win_qkv, h_win_out, h_win_up, h_win_down, h_mem_qkv, h_mem_out,
    h_shift_qkv, h_shift_out, h_shift_up, h_shift_down,
    out,
    fields, win_qkv, win_out, win_up, win_down, mem_qkv, mem_out,
    shift_qkv, shift_out, shift_up, shift_down,
    stream, mine, got, qkv, mixed, mixed_send, mixed_got,
    late, vert, left, right, corner, corner_left, corner_right,
    w_sem, a_send, a_recv, r_send, r_recv, v_send, v_recv,
    l_send, l_recv, rt_send, rt_recv, c_send, c_recv,
):
    n_member, n_lat, n_lon = sizes
    members = h_fields.shape[0]
    channels = h_fields.shape[-1]
    tokens = WIN * WIN
    part = tokens // 2
    edge, inner = 0, 1
    me = lax.axis_index("member")
    lat = lax.axis_index("lat")
    lon = lax.axis_index("lon")
    core = lax.rem(me, 2)
    chip = me // 2
    other = 1 - core
    mate = {"member": 2 * chip + other}
    far_same = {"member": 2 * (1 - chip) + core}
    far_other = {"member": 2 * (1 - chip) + other}
    lat_up = {"lat": lax.rem(lat + n_lat - 1, n_lat)}
    lat_down = {"lat": lax.rem(lat + 1, n_lat)}
    lon_left = {"lon": lax.rem(lon + n_lon - 1, n_lon)}
    lon_right = {"lon": lax.rem(lon + 1, n_lon)}

    barrier = pltpu.get_barrier_semaphore()
    for peer in (mate, far_same, far_other, lat_up, lat_down, lon_left, lon_right):
        pl.semaphore_signal(barrier, inc=1, device_id=peer, device_id_type=MESH)

    pairs = [
        (h_fields, fields),
        (h_win_qkv, win_qkv), (h_win_out, win_out), (h_win_up, win_up),
        (h_win_down, win_down), (h_mem_qkv, mem_qkv), (h_mem_out, mem_out),
        (h_shift_qkv, shift_qkv), (h_shift_out, shift_out),
        (h_shift_up, shift_up), (h_shift_down, shift_down),
    ]
    loads = [
        pltpu.make_async_copy(source, target, w_sem.at[i])
        for i, (source, target) in enumerate(pairs)
    ]
    for load in loads:
        load.start()

    off0 = offsets[0]
    off1 = offsets[1]
    split0 = WIN - off0
    split1 = WIN - off1
    masks_bf = head_masks(channels, BF)
    masks_f32 = head_masks(channels, F32)
    scale = (channels // HEADS) ** -0.5

    def push(source, target, send, recv, peer):
        copy = pltpu.make_async_remote_copy(
            src_ref=source, dst_ref=target, send_sem=send, recv_sem=recv,
            device_id=peer, device_id_type=MESH,
        )
        copy.start()
        return copy

    token = lax.broadcasted_iota(jnp.int32, (tokens, channels), 0)
    is_low = token // WIN < split0
    row_low = jnp.where(is_low, 1.0, 0.0)
    col_low = jnp.where(lax.rem(token, WIN) < split1, 1.0, 0.0)

    flags = pltpu.roll(land[...].astype(F32), split1, 0)
    spread = jnp.concatenate([flags] * (2 * WIN), axis=0)
    s_row = lax.broadcasted_iota(jnp.int32, spread.shape, 0) // WIN
    s_lane = lax.broadcasted_iota(jnp.int32, spread.shape, 1)
    s_pick = WIN * (s_row // WIN) + lax.rem(lax.rem(s_row, WIN) + off0, WIN)
    is_land = jnp.sum(jnp.where(s_lane == s_pick, spread, 0.0), axis=-1, keepdims=True)
    added = is_land * embed[...]
    rows = [WIN * b + lax.rem(s + off0, WIN) for b in range(2) for s in range(WIN)]

    loads[0].wait()

    def window_section(m):
        tile = jnp.concatenate(
            [fields[m, r].astype(F32).reshape(1, WIN, channels) for r in rows], axis=0
        )
        x = pltpu.roll(tile, split1, 1).reshape(2 * tokens, channels) + added
        if m == 0:
            loads[1].wait()
        proj = project(normalize(x), win_qkv[...])
        atts = []
        for b in range(2):
            span = slice(b * tokens, (b + 1) * tokens)
            q = (proj[span, :channels] * scale).astype(BF)
            k = proj[span, channels : 2 * channels].astype(BF)
            v = proj[span, 2 * channels :].astype(BF)
            atts.append(attend(q, k, v, None, masks_bf, masks_f32))
        if m == 0:
            loads[2].wait()
        x = x + project(jnp.concatenate(atts, axis=0).astype(BF), win_out[...])
        if m == 0:
            loads[3].wait()
            loads[4].wait()
        x = feed_forward(x, win_up[...], win_down[...])
        top, bottom = x[:tokens], x[tokens:]
        tiles = [jnp.where(is_low, bottom, top), jnp.where(is_low, top, bottom)]
        for e in range(2):
            normed = normalize(tiles[e])
            for half in range(2):
                span = slice(half * part, (half + 1) * part)
                stream[e, half, m] = tiles[e][span].reshape(WIN // 2, WIN, channels)
                mine[e, half, m] = normed[span]

    sends = {}

    def send_members(e, m):
        for i, (half, peer) in enumerate(
            ((other, mate), (other, far_other), (core, far_same))
        ):
            sends[i, e, m] = push(
                mine.at[e, half, m], got.at[i, e, m], a_send.at[i, e, m],
                a_recv.at[i, e, m], peer,
            )

    window_section(0)
    pl.semaphore_wait(barrier, 7)
    send_members(edge, 0)
    window_section(1)
    send_members(edge, 1)
    send_members(inner, 0)
    window_section(2)
    send_members(edge, 2)
    send_members(inner, 1)
    send_members(inner, 2)

    near = 2 * members
    total = 4 * members
    qt = lax.rem(lax.broadcasted_iota(jnp.int32, (near * WIN, total * WIN), 0), WIN)
    kt = lax.rem(lax.broadcasted_iota(jnp.int32, (near * WIN, total * WIN), 1), WIN)
    same_token = jnp.where(qt == kt, 0.0, NEG)
    backs = []

    def member_qkv(source, x, with_q):
        weights = mem_qkv[...] if with_q else mem_qkv[:, channels:]
        first_col = 0 if with_q else channels
        qkv[source, :, :, first_col:] = project(
            x.reshape(members * part, channels), weights
        ).reshape(members, part, -1)

    def member_attention(e):
        member_qkv(0, mine[e, core], True)
        for m in range(members):
            sends[0, e, m].wait_recv()
        member_qkv(1, got[0, e], True)
        for i in (1, 2):
            for m in range(members):
                sends[i, e, m].wait_recv()
            member_qkv(i + 1, got[i, e], False)
        for group in range(part // WIN):
            span = slice(group * WIN, (group + 1) * WIN)
            q = qkv[0:2, :, span, 0:channels].reshape(near * WIN, channels)
            k = qkv[:, :, span, channels : 2 * channels].reshape(total * WIN, channels)
            v = qkv[:, :, span, 2 * channels :].reshape(total * WIN, channels)
            att = attend(
                (q * scale).astype(BF), k.astype(BF), v.astype(BF), same_token,
                masks_bf, masks_f32,
            )
            mixed[:, :, span, :] = att.reshape(2, members, WIN, channels)
        mixed_send[e] = mixed[1].astype(BF)
        backs.append(
            push(mixed_send.at[e], mixed_got.at[e], r_send.at[e], r_recv.at[e], mate)
        )

    def member_add(e, half, att):
        x = stream[e, half].reshape(members * part, channels)
        x = x + project(att.reshape(members * part, channels), mem_out[...])
        stream[e, half] = x.reshape(members, WIN // 2, WIN, channels)
        late[e, half] = normalize(x).reshape(members, part, channels)

    halo = []

    def send_lat(half):
        piece = late.at[edge, half]
        halo.append(push(piece, vert.at[1, half], v_send.at[1, half], v_recv.at[1, half], lat_up))
        halo.append(push(piece, vert.at[0, half], v_send.at[0, half], v_recv.at[0, half], lat_down))

    def send_lon(e, half):
        piece = late.at[e, half]
        halo.append(push(piece, right.at[e, half], l_send.at[e, half], l_recv.at[e, half], lon_left))
        halo.append(push(piece, left.at[e, half], rt_send.at[e, half], rt_recv.at[e, half], lon_right))

    def arrived(buffer, sem):
        pltpu.make_async_copy(buffer, buffer, sem).wait()

    loads[5].wait()
    loads[6].wait()
    member_attention(edge)
    member_add(edge, core, mixed[0].astype(BF))
    send_lat(core)
    send_lon(edge, core)
    arrived(mixed_got.at[edge], r_recv.at[edge])
    member_add(edge, other, mixed_got[edge])
    send_lat(other)
    send_lon(edge, other)
    member_attention(inner)
    member_add(inner, core, mixed[0].astype(BF))
    send_lon(inner, core)
    arrived(mixed_got.at[inner], r_recv.at[inner])
    member_add(inner, other, mixed_got[inner])
    send_lon(inner, other)

    mr, nr = row_low.astype(BF), (1.0 - row_low).astype(BF)
    mc, nc = col_low.astype(BF), (1.0 - col_low).astype(BF)
    for half in (core, other):
        arrived(vert.at[0, half], v_recv.at[0, half])
        arrived(vert.at[1, half], v_recv.at[1, half])
        h_tok = lax.broadcasted_iota(jnp.int32, (part, channels), 0) + half * part
        h_low = jnp.where(h_tok // WIN < split0, 1.0, 0.0)
        h_mr, h_nr = h_low.astype(BF), (1.0 - h_low).astype(BF)
        corner[half] = vert[0, half] * h_mr[None] + vert[1, half] * h_nr[None]
        halo.append(
            push(corner.at[half], corner_right.at[half], c_send.at[0, half],
                 c_recv.at[0, half], lon_left)
        )
        halo.append(
            push(corner.at[half], corner_left.at[half], c_send.at[1, half],
                 c_recv.at[1, half], lon_right)
        )

    q_tok = lax.broadcasted_iota(jnp.int32, (tokens, 4 * tokens), 0)
    k_tok = lax.broadcasted_iota(jnp.int32, (tokens, 4 * tokens), 1)
    q_row = jnp.where(q_tok // WIN < split0, 1, 0)
    q_col = jnp.where(lax.rem(q_tok, WIN) < split1, 1, 0)
    k_row = k_tok // (2 * tokens)
    k_col = lax.rem(k_tok // tokens, 2)
    k_low = jnp.where(lax.rem(k_tok, tokens) // WIN < split0, 1, 0)
    col_bias = jnp.where(q_col == k_col, 0.0, NEG)
    first = jnp.where(lat == 0, 1.0, 0.0)
    last = jnp.where(lat == n_lat - 1, 1.0, 0.0)
    outside = jnp.where(k_row == 0, jnp.where(k_low == 1, NEG, 0.0), 0.0) * first
    outside = outside + jnp.where(k_row == 1, jnp.where(k_low == 0, NEG, 0.0), 0.0) * last
    edge_bias = jnp.where(q_row == k_row, 0.0, NEG) + col_bias + outside
    inner_bias = col_bias[:, : 2 * tokens]

    for load in loads[7:]:
        load.wait()

    def whole(ref, m):
        return ref[:, m].reshape(tokens, channels)

    def finish(e, windows, bias):
        count = len(windows[0]) * tokens
        own = jnp.concatenate([whole(late.at[e], m) for m in range(members)], axis=0)
        asked = (project(own, shift_qkv[:, :channels]) * scale).astype(BF)
        keyed = project(
            jnp.concatenate([w for group in windows for w in group], axis=0),
            shift_qkv[:, channels:],
        ).astype(BF)
        atts = []
        for m in range(members):
            keys = slice(m * count, (m + 1) * count)
            atts.append(
                attend(
                    asked[m * tokens : (m + 1) * tokens], keyed[keys, :channels],
                    keyed[keys, channels:], bias, masks_bf, masks_f32,
                )
            )
        x = jnp.concatenate(
            [stream[e, :, m].reshape(tokens, channels) for m in range(members)], axis=0
        )
        x = x + project(jnp.concatenate(atts, axis=0).astype(BF), shift_out[...])
        x = feed_forward(x, shift_up[...], shift_down[...])
        for m in range(members):
            stream[e, :, m] = x[m * tokens : (m + 1) * tokens].reshape(
                2, WIN // 2, WIN, channels
            )

    for half in range(2):
        arrived(right.at[inner, half], l_recv.at[inner, half])
        arrived(left.at[inner, half], rt_recv.at[inner, half])
    windows = []
    for m in range(members):
        own = whole(late.at[inner], m)
        windows.append(
            [
                whole(left.at[inner], m) * mc + own * nc,
                own * mc + whole(right.at[inner], m) * nc,
            ]
        )
    finish(inner, windows, inner_bias)

    for half in range(2):
        arrived(right.at[edge, half], l_recv.at[edge, half])
        arrived(left.at[edge, half], rt_recv.at[edge, half])
    for half in range(2):
        arrived(corner_right.at[half], c_recv.at[0, half])
        arrived(corner_left.at[half], c_recv.at[1, half])
    windows = []
    for m in range(members):
        own = whole(late.at[edge], m)
        beyond = whole(corner, m)
        side = whole(left.at[edge], m) * mc + whole(right.at[edge], m) * nc
        far = whole(corner_left, m) * mc + whole(corner_right, m) * nc
        group = []
        for middle, flank in (
            (beyond * mr + own * nr, far * mr + side * nr),
            (own * mr + beyond * nr, side * mr + far * nr),
        ):
            group.append(flank * mc + middle * nc)
            group.append(middle * mc + flank * nc)
        windows.append(group)
    finish(edge, windows, edge_bias)

    for b in range(2):
        spots = []
        for r in range(WIN):
            place = lax.rem(r + split0, WIN)
            low = jnp.where(place < split0, 1, 0)
            tile_of = low if b == 0 else 1 - low
            spots.append((tile_of, place // (WIN // 2), lax.rem(place, WIN // 2)))
        for m in range(members):
            tile = jnp.concatenate(
                [stream[t, h, m, p].reshape(1, WIN, channels) for t, h, p in spots], axis=0
            )
            tile = pltpu.roll(tile, off1, 1)
            out[m, b * WIN : (b + 1) * WIN] = tile.astype(BF)

    for copy in list(sends.values()) + backs + halo:
        copy.wait_send()


def per_device(sizes, fields, land_mask, offsets, land_embed, *weights):
    members, height, breadth, channels = fields.shape
    tokens = WIN * WIN
    part = tokens // 2
    vmem = pl.BlockSpec(memory_space=pltpu.VMEM)
    hbm = pl.BlockSpec(memory_space=pltpu.HBM)
    piece = (members, part, channels)
    dma = pltpu.SemaphoreType.DMA
    scratch = [pltpu.VMEM(w.shape, w.dtype) for w in (fields,) + weights] + [
        pltpu.VMEM((2, 2, members, WIN // 2, WIN, channels), F32),
        pltpu.VMEM((2, 2) + piece, BF),
        pltpu.VMEM((3, 2) + piece, BF),
        pltpu.VMEM((4, members, part, 3 * channels), F32),
        pltpu.VMEM((2,) + piece, F32),
        pltpu.VMEM((2,) + piece, BF),
        pltpu.VMEM((2,) + piece, BF),
        pltpu.VMEM((2, 2) + piece, BF),
        pltpu.VMEM((2, 2) + piece, BF),
        pltpu.VMEM((2, 2) + piece, BF),
        pltpu.VMEM((2, 2) + piece, BF),
        pltpu.VMEM((2,) + piece, BF),
        pltpu.VMEM((2,) + piece, BF),
        pltpu.VMEM((2,) + piece, BF),
        dma((len(weights) + 1,)),
        dma((3, 2, members)), dma((3, 2, members)), dma((2,)), dma((2,)),
        dma((2, 2)), dma((2, 2)),
        dma((2, 2)), dma((2, 2)),
        dma((2, 2)), dma((2, 2)),
        dma((2, 2)), dma((2, 2)),
    ]
    return pl.pallas_call(
        functools.partial(kernel, sizes),
        out_shape=pltpu.VMEM(fields.shape, BF),
        in_specs=[hbm, vmem, pl.BlockSpec(memory_space=pltpu.SMEM), vmem]
        + [hbm] * len(weights),
        out_specs=vmem,
        scratch_shapes=scratch,
        compiler_params=pltpu.CompilerParams(collective_id=0, has_side_effects=True, vmem_limit_bytes=VMEM_LIMIT),
        name="scorer",
    )(fields, land_mask.T, offsets, land_embed.reshape(1, channels), *weights)


def solution(mesh):
    sizes = tuple(mesh.shape[axis] for axis in ("member", "lat", "lon"))
    return jax.shard_map(
        functools.partial(per_device, sizes),
        mesh=mesh,
        in_specs=(P("member", "lat", "lon", None), P("lat", "lon")) + (P(),) * 12,
        out_specs=P("member", "lat", "lon", None),
        check_vma=False,
    )
```

time: 40.5 us -> 37 us (0.914)
  local copies, waits for them, and re-layouts: 2.97 us -> 0.68 us
  Pallas kernels: 37.4 us -> 36.2 us
    unnamed x2 -> x1, local copies, waits for them, and re-layouts: 2.97 us -> 0.68 us
    pallas_call x1, Pallas kernels: 37.4 us -> 36.2 us  [per_device(): pl.pallas_call(functools.partial(kernel, sizes), out_shape=pltpu.VMEM(fie...]
where the time goes in v2:
time: 37 us; the launch traced here: 36.9 us
  Pallas kernels  36.2 us (98%)
  local copies, waits for them, and re-layouts  0.68 us (2%)
    pallas_call x1, Pallas kernels, per_device(): pl.pallas_call(functools.partial(kernel, sizes), out_shape=pltpu.VMEM(fie...  36.2 us

profile of v2, /device:TPU:1, one launch (start us, length us, event | category | flops | bytes accessed | tf_op | source)
XLA Modules:
  0.0 36.9 jit_solution(5569376359448246928)
XLA Ops:
  0.0 36.2 %scorer.1 = bf16[3,16,8,256]{3,2,1,0:T(8,128)(2,1)S(1)} custom-call(bf16[3,16,8,256]{3,2,1,0:T(8,128)(2,1)} %h_fields.1, s32[8,16]{1,0:T(8,128)} %bitcast.2, s32[2]{0:T(128)} %offsets.1, f32[1,256]{1,0:T(1,128)} %bitcast.3, bf16[256,768]{1,0:T(8,128)(2,1)} %h_win_qkv.1, bf16[256,256]{1,0:T(8,128)(2,1)} %h_win_out.1, bf16[256,1024]{1,0:T(8,128)(2,1)} %h_win_up.1, ...), custom_call_target="tpu_custom_call" | custom-call | tf_op jit(solution)/shard_map/scorer/pallas_call | solution.py:428
  36.2 0.7 %copy.16 = bf16[3,16,8,256]{3,2,1,0:T(8,128)(2,1)} copy(bf16[3,16,8,256]{3,2,1,0:T(8,128)(2,1)S(1)} %scorer.1) | data formatting | bytes 393216

commit v3 on v2

--- a/solution.py
+++ b/solution.py
@@ -72,7 +72,7 @@
     fields, win_qkv, win_out, win_up, win_down, mem_qkv, mem_out,
     shift_qkv, shift_out, shift_up, shift_down,
     stream, mine, got, qkv, mixed, mixed_send, mixed_got,
-    late, vert, left, right, corner, corner_left, corner_right,
+    late, vert, left, right, corner, corner_left, corner_right, final,
     w_sem, a_send, a_recv, r_send, r_recv, v_send, v_recv,
     l_send, l_recv, rt_send, rt_recv, c_send, c_recv,
 ):
@@ -136,68 +136,65 @@
     col_low = jnp.where(lax.rem(token, WIN) < split1, 1.0, 0.0)
 
     flags = pltpu.roll(land[...].astype(F32), split1, 0)
-    spread = jnp.concatenate([flags] * (2 * WIN), axis=0)
+    spread = jnp.concatenate([flags] * WIN, axis=0)
     s_row = lax.broadcasted_iota(jnp.int32, spread.shape, 0) // WIN
     s_lane = lax.broadcasted_iota(jnp.int32, spread.shape, 1)
-    s_pick = WIN * (s_row // WIN) + lax.rem(lax.rem(s_row, WIN) + off0, WIN)
-    is_land = jnp.sum(jnp.where(s_lane == s_pick, spread, 0.0), axis=-1, keepdims=True)
-    added = is_land * embed[...]
-    rows = [WIN * b + lax.rem(s + off0, WIN) for b in range(2) for s in range(WIN)]
-
+    s_pick = lax.rem(s_row + off0, WIN)
     loads[0].wait()
 
-    def window_section(m):
-        tile = jnp.concatenate(
-            [fields[m, r].astype(F32).reshape(1, WIN, channels) for r in rows], axis=0
-        )
-        x = pltpu.roll(tile, split1, 1).reshape(2 * tokens, channels) + added
-        if m == 0:
+    def window_section(block, waits):
+        rows = [WIN * block + lax.rem(s + off0, WIN) for s in range(WIN)]
+        picked = jnp.where(s_lane == WIN * block + s_pick, spread, 0.0)
+        added = jnp.sum(picked, axis=-1, keepdims=True) * embed[...]
+        tiles = []
+        for m in range(members):
+            tile = jnp.concatenate(
+                [fields[m, r].astype(F32).reshape(1, WIN, channels) for r in rows], axis=0
+            )
+            tiles.append(pltpu.roll(tile, split1, 1).reshape(tokens, channels) + added)
+        x = jnp.concatenate(tiles, axis=0)
+        if waits:
             loads[1].wait()
         proj = project(normalize(x), win_qkv[...])
         atts = []
-        for b in range(2):
-            span = slice(b * tokens, (b + 1) * tokens)
+        for m in range(members):
+            span = slice(m * tokens, (m + 1) * tokens)
             q = (proj[span, :channels] * scale).astype(BF)
             k = proj[span, channels : 2 * channels].astype(BF)
             v = proj[span, 2 * channels :].astype(BF)
             atts.append(attend(q, k, v, None, masks_bf, masks_f32))
-        if m == 0:
+        if waits:
             loads[2].wait()
         x = x + project(jnp.concatenate(atts, axis=0).astype(BF), win_out[...])
-        if m == 0:
+        if waits:
             loads[3].wait()
             loads[4].wait()
         x = feed_forward(x, win_up[...], win_down[...])
-        top, bottom = x[:tokens], x[tokens:]
-        tiles = [jnp.where(is_low, bottom, top), jnp.where(is_low, top, bottom)]
-        for e in range(2):
-            normed = normalize(tiles[e])
+        normed = normalize(x)
+        for m in range(members):
             for half in range(2):
-                span = slice(half * part, (half + 1) * part)
-                stream[e, half, m] = tiles[e][span].reshape(WIN // 2, WIN, channels)
-                mine[e, half, m] = normed[span]
+                first = m * tokens + half * part
+                span = slice(first, first + part)
+                stream[block, half, m] = x[span].reshape(WIN // 2, WIN, channels)
+                mine[block, half, m] = normed[span]
 
     sends = {}
 
-    def send_members(e, m):
-        for i, (half, peer) in enumerate(
-            ((other, mate), (other, far_other), (core, far_same))
-        ):
-            sends[i, e, m] = push(
-                mine.at[e, half, m], got.at[i, e, m], a_send.at[i, e, m],
-                a_recv.at[i, e, m], peer,
-            )
-
-    window_section(0)
+    def send_members(block, i, peer):
+        for half in range(2):
+            sends[i, half] = push(
+                mine.at[block, half], got.at[i, half], a_send.at[i, half],
+                a_recv.at[i, half], peer,
+            )
+
+    window_section(other, True)
     pl.semaphore_wait(barrier, 7)
-    send_members(edge, 0)
-    window_section(1)
-    send_members(edge, 1)
-    send_members(inner, 0)
-    window_section(2)
-    send_members(edge, 2)
-    send_members(inner, 1)
-    send_members(inner, 2)
+    send_members(other, 1, far_other)
+    send_members(other, 0, mate)
+    window_section(core, False)
+    send_members(core, 2, far_same)
+    loads[5].wait()
+    loads[6].wait()
 
     near = 2 * members
     total = 4 * members
@@ -214,13 +211,11 @@
         ).reshape(members, part, -1)
 
     def member_attention(e):
-        member_qkv(0, mine[e, core], True)
-        for m in range(members):
-            sends[0, e, m].wait_recv()
+        member_qkv(0, mine[core, e], True)
+        sends[0, e].wait_recv()
         member_qkv(1, got[0, e], True)
         for i in (1, 2):
-            for m in range(members):
-                sends[i, e, m].wait_recv()
+            sends[i, e].wait_recv()
             member_qkv(i + 1, got[i, e], False)
         for group in range(part // WIN):
             span = slice(group * WIN, (group + 1) * WIN)
@@ -245,39 +240,32 @@
 
     halo = []
 
-    def send_lat(half):
-        piece = late.at[edge, half]
-        halo.append(push(piece, vert.at[1, half], v_send.at[1, half], v_recv.at[1, half], lat_up))
-        halo.append(push(piece, vert.at[0, half], v_send.at[0, half], v_recv.at[0, half], lat_down))
-
-    def send_lon(e, half):
-        piece = late.at[e, half]
-        halo.append(push(piece, right.at[e, half], l_send.at[e, half], l_recv.at[e, half], lon_left))
-        halo.append(push(piece, left.at[e, half], rt_send.at[e, half], rt_recv.at[e, half], lon_right))
+    def send_halo(block, half):
+        piece = late.at[block, half]
+        toward = {"lat": lax.rem(lat + 2 * block - 1 + n_lat, n_lat)}
+        for target, send, recv, peer in (
+            (vert.at[1 - block, half], v_send.at[block, half], v_recv.at[1 - block, half], toward),
+            (right.at[block, half], l_send.at[block, half], l_recv.at[block, half], lon_left),
+            (left.at[block, half], rt_send.at[block, half], rt_recv.at[block, half], lon_right),
+        ):
+            halo.append(push(piece, target, send, recv, peer))
 
     def arrived(buffer, sem):
         pltpu.make_async_copy(buffer, buffer, sem).wait()
 
-    loads[5].wait()
-    loads[6].wait()
-    member_attention(edge)
-    member_add(edge, core, mixed[0].astype(BF))
-    send_lat(core)
-    send_lon(edge, core)
-    arrived(mixed_got.at[edge], r_recv.at[edge])
-    member_add(edge, other, mixed_got[edge])
-    send_lat(other)
-    send_lon(edge, other)
-    member_attention(inner)
-    member_add(inner, core, mixed[0].astype(BF))
-    send_lon(inner, core)
-    arrived(mixed_got.at[inner], r_recv.at[inner])
-    member_add(inner, other, mixed_got[inner])
-    send_lon(inner, other)
+    for half in range(2):
+        member_attention(half)
+        member_add(core, half, mixed[0].astype(BF))
+        send_halo(core, half)
+    for half in range(2):
+        arrived(mixed_got.at[half], r_recv.at[half])
+        member_add(other, half, mixed_got[half])
+        send_halo(other, half)
 
     mr, nr = row_low.astype(BF), (1.0 - row_low).astype(BF)
     mc, nc = col_low.astype(BF), (1.0 - col_low).astype(BF)
-    for half in (core, other):
+
+    def relay(half):
         arrived(vert.at[0, half], v_recv.at[0, half])
         arrived(vert.at[1, half], v_recv.at[1, half])
         h_tok = lax.broadcasted_iota(jnp.int32, (part, channels), 0) + half * part
@@ -292,6 +280,9 @@
             push(corner.at[half], corner_left.at[half], c_send.at[1, half],
                  c_recv.at[1, half], lon_right)
         )
+
+    relay(0)
+    relay(1)
 
     q_tok = lax.broadcasted_iota(jnp.int32, (tokens, 4 * tokens), 0)
     k_tok = lax.broadcasted_iota(jnp.int32, (tokens, 4 * tokens), 1)
@@ -314,9 +305,12 @@
     def whole(ref, m):
         return ref[:, m].reshape(tokens, channels)
 
+    def joined(ref, e, m):
+        return whole(ref.at[1 - e], m) * mr + whole(ref.at[e], m) * nr
+
     def finish(e, windows, bias):
         count = len(windows[0]) * tokens
-        own = jnp.concatenate([whole(late.at[e], m) for m in range(members)], axis=0)
+        own = jnp.concatenate([joined(late, e, m) for m in range(members)], axis=0)
         asked = (project(own, shift_qkv[:, :channels]) * scale).astype(BF)
         keyed = project(
             jnp.concatenate([w for group in windows for w in group], axis=0),
@@ -332,40 +326,46 @@
                 )
             )
         x = jnp.concatenate(
-            [stream[e, :, m].reshape(tokens, channels) for m in range(members)], axis=0
+            [
+                jnp.where(
+                    is_low,
+                    stream[1 - e, :, m].reshape(tokens, channels),
+                    stream[e, :, m].reshape(tokens, channels),
+                )
+                for m in range(members)
+            ],
+            axis=0,
         )
         x = x + project(jnp.concatenate(atts, axis=0).astype(BF), shift_out[...])
         x = feed_forward(x, shift_up[...], shift_down[...])
         for m in range(members):
-            stream[e, :, m] = x[m * tokens : (m + 1) * tokens].reshape(
+            final[e, :, m] = x[m * tokens : (m + 1) * tokens].reshape(
                 2, WIN // 2, WIN, channels
             )
 
-    for half in range(2):
-        arrived(right.at[inner, half], l_recv.at[inner, half])
-        arrived(left.at[inner, half], rt_recv.at[inner, half])
+    for block in range(2):
+        for half in range(2):
+            arrived(right.at[block, half], l_recv.at[block, half])
+            arrived(left.at[block, half], rt_recv.at[block, half])
     windows = []
     for m in range(members):
-        own = whole(late.at[inner], m)
+        own = joined(late, inner, m)
         windows.append(
             [
-                whole(left.at[inner], m) * mc + own * nc,
-                own * mc + whole(right.at[inner], m) * nc,
+                joined(left, inner, m) * mc + own * nc,
+                own * mc + joined(right, inner, m) * nc,
             ]
         )
     finish(inner, windows, inner_bias)
 
-    for half in range(2):
-        arrived(right.at[edge, half], l_recv.at[edge, half])
-        arrived(left.at[edge, half], rt_recv.at[edge, half])
     for half in range(2):
         arrived(corner_right.at[half], c_recv.at[0, half])
         arrived(corner_left.at[half], c_recv.at[1, half])
     windows = []
     for m in range(members):
-        own = whole(late.at[edge], m)
+        own = joined(late, edge, m)
         beyond = whole(corner, m)
-        side = whole(left.at[edge], m) * mc + whole(right.at[edge], m) * nc
+        side = joined(left, edge, m) * mc + joined(right, edge, m) * nc
         far = whole(corner_left, m) * mc + whole(corner_right, m) * nc
         group = []
         for middle, flank in (
@@ -386,7 +386,7 @@
             spots.append((tile_of, place // (WIN // 2), lax.rem(place, WIN // 2)))
         for m in range(members):
             tile = jnp.concatenate(
-                [stream[t, h, m, p].reshape(1, WIN, channels) for t, h, p in spots], axis=0
+                [final[t, h, m, p].reshape(1, WIN, channels) for t, h, p in spots], axis=0
             )
             tile = pltpu.roll(tile, off1, 1)
             out[m, b * WIN : (b + 1) * WIN] = tile.astype(BF)
@@ -418,8 +418,9 @@
         pltpu.VMEM((2,) + piece, BF),
         pltpu.VMEM((2,) + piece, BF),
         pltpu.VMEM((2,) + piece, BF),
+        pltpu.VMEM((2, 2, members, WIN // 2, WIN, channels), F32),
         dma((len(weights) + 1,)),
-        dma((3, 2, members)), dma((3, 2, members)), dma((2,)), dma((2,)),
+        dma((3, 2)), dma((3, 2)), dma((2,)), dma((2,)),
         dma((2, 2)), dma((2, 2)),
         dma((2, 2)), dma((2, 2)),
         dma((2, 2)), dma((2, 2)),

time: 37 us -> 35.1 us (0.949); the launches traced: 36.9 us -> 34.4 us
  Pallas kernels: 36.2 us -> 33.7 us
    pallas_call x1, Pallas kernels: 36.2 us -> 33.7 us  [per_device(): pl.pallas_call(functools.partial(kernel, sizes), out_shape=pltpu.VMEM(fie...]
where the time goes in v3:
time: 35.1 us; the launch traced here: 34.4 us
  Pallas kernels  33.7 us (96%)
  local copies, waits for them, and re-layouts  0.68 us (2%)
    pallas_call x1, Pallas kernels, per_device(): pl.pallas_call(functools.partial(kernel, sizes), out_shape=pltpu.VMEM(fie...  33.7 us

profile of v3, /device:TPU:1, one launch (start us, length us, event | category | flops | bytes accessed | tf_op | source)
XLA Modules:
  0.0 34.4 jit_solution(17274564766146597304)
XLA Ops:
  0.0 33.7 %scorer.1 = bf16[3,16,8,256]{3,2,1,0:T(8,128)(2,1)S(1)} custom-call(bf16[3,16,8,256]{3,2,1,0:T(8,128)(2,1)} %h_fields.1, s32[8,16]{1,0:T(8,128)} %bitcast.2, s32[2]{0:T(128)} %offsets.1, f32[1,256]{1,0:T(1,128)} %bitcast.3, bf16[256,768]{1,0:T(8,128)(2,1)} %h_win_qkv.1, bf16[256,256]{1,0:T(8,128)(2,1)} %h_win_out.1, bf16[256,1024]{1,0:T(8,128)(2,1)} %h_win_up.1, ...), custom_call_target="tpu_custom_call" | custom-call | tf_op jit(solution)/shard_map/scorer/pallas_call | solution.py:429
  33.7 0.7 %copy.16 = bf16[3,16,8,256]{3,2,1,0:T(8,128)(2,1)} copy(bf16[3,16,8,256]{3,2,1,0:T(8,128)(2,1)S(1)} %scorer.1) | data formatting | bytes 393216

commit v4 on v3

--- a/solution.py
+++ b/solution.py
@@ -180,19 +180,20 @@
 
     sends = {}
 
-    def send_members(block, i, peer):
-        for half in range(2):
-            sends[i, half] = push(
-                mine.at[block, half], got.at[i, half], a_send.at[i, half],
-                a_recv.at[i, half], peer,
-            )
-
-    window_section(other, True)
+    def send_members(block):
+        for i, (half, peer) in enumerate(
+            ((other, mate), (other, far_other), (core, far_same))
+        ):
+            sends[i, block] = push(
+                mine.at[block, half], got.at[i, block], a_send.at[i, block],
+                a_recv.at[i, block], peer,
+            )
+
+    window_section(0, True)
     pl.semaphore_wait(barrier, 7)
-    send_members(other, 1, far_other)
-    send_members(other, 0, mate)
-    window_section(core, False)
-    send_members(core, 2, far_same)
+    send_members(0)
+    window_section(1, False)
+    send_members(1)
     loads[5].wait()
     loads[6].wait()
 
@@ -211,7 +212,7 @@
         ).reshape(members, part, -1)
 
     def member_attention(e):
-        member_qkv(0, mine[core, e], True)
+        member_qkv(0, mine[e, core], True)
         sends[0, e].wait_recv()
         member_qkv(1, got[0, e], True)
         for i in (1, 2):
@@ -253,14 +254,13 @@
     def arrived(buffer, sem):
         pltpu.make_async_copy(buffer, buffer, sem).wait()
 
-    for half in range(2):
-        member_attention(half)
-        member_add(core, half, mixed[0].astype(BF))
-        send_halo(core, half)
-    for half in range(2):
-        arrived(mixed_got.at[half], r_recv.at[half])
-        member_add(other, half, mixed_got[half])
-        send_halo(other, half)
+    for block in range(2):
+        member_attention(block)
+        member_add(block, core, mixed[0].astype(BF))
+        send_halo(block, core)
+        arrived(mixed_got.at[block], r_recv.at[block])
+        member_add(block, other, mixed_got[block])
+        send_halo(block, other)
 
     mr, nr = row_low.astype(BF), (1.0 - row_low).astype(BF)
     mc, nc = col_low.astype(BF), (1.0 - col_low).astype(BF)
@@ -281,8 +281,8 @@
                  c_recv.at[1, half], lon_right)
         )
 
-    relay(0)
-    relay(1)
+    relay(core)
+    relay(other)
 
     q_tok = lax.broadcasted_iota(jnp.int32, (tokens, 4 * tokens), 0)
     k_tok = lax.broadcasted_iota(jnp.int32, (tokens, 4 * tokens), 1)
@@ -308,24 +308,17 @@
     def joined(ref, e, m):
         return whole(ref.at[1 - e], m) * mr + whole(ref.at[e], m) * nr
 
-    def finish(e, windows, bias):
-        count = len(windows[0]) * tokens
-        own = jnp.concatenate([joined(late, e, m) for m in range(members)], axis=0)
-        asked = (project(own, shift_qkv[:, :channels]) * scale).astype(BF)
-        keyed = project(
-            jnp.concatenate([w for group in windows for w in group], axis=0),
-            shift_qkv[:, channels:],
-        ).astype(BF)
-        atts = []
-        for m in range(members):
-            keys = slice(m * count, (m + 1) * count)
-            atts.append(
-                attend(
-                    asked[m * tokens : (m + 1) * tokens], keyed[keys, :channels],
-                    keyed[keys, channels:], bias, masks_bf, masks_f32,
-                )
-            )
-        x = jnp.concatenate(
+    def stacked(pieces):
+        return jnp.concatenate(pieces, axis=0)
+
+    def ask(owns):
+        return (project(stacked(owns), shift_qkv[:, :channels]) * scale).astype(BF)
+
+    def to_keyed(pieces):
+        return project(stacked(pieces), shift_qkv[:, channels:]).astype(BF)
+
+    def residual(e):
+        return stacked(
             [
                 jnp.where(
                     is_low,
@@ -333,10 +326,19 @@
                     stream[e, :, m].reshape(tokens, channels),
                 )
                 for m in range(members)
-            ],
-            axis=0,
+            ]
         )
-        x = x + project(jnp.concatenate(atts, axis=0).astype(BF), shift_out[...])
+
+    def finish(e, x, asked, keyed, bias):
+        atts = []
+        for m in range(members):
+            atts.append(
+                attend(
+                    asked[m * tokens : (m + 1) * tokens], keyed[m][:, :channels],
+                    keyed[m][:, channels:], bias, masks_bf, masks_f32,
+                )
+            )
+        x = x + project(stacked(atts).astype(BF), shift_out[...])
         x = feed_forward(x, shift_up[...], shift_down[...])
         for m in range(members):
             final[e, :, m] = x[m * tokens : (m + 1) * tokens].reshape(
@@ -347,35 +349,50 @@
         for half in range(2):
             arrived(right.at[block, half], l_recv.at[block, half])
             arrived(left.at[block, half], rt_recv.at[block, half])
+    owns = [joined(late, inner, m) for m in range(members)]
     windows = []
     for m in range(members):
-        own = joined(late, inner, m)
-        windows.append(
-            [
-                joined(left, inner, m) * mc + own * nc,
-                own * mc + joined(right, inner, m) * nc,
-            ]
-        )
-    finish(inner, windows, inner_bias)
-
+        windows.append(joined(left, inner, m) * mc + owns[m] * nc)
+        windows.append(owns[m] * mc + joined(right, inner, m) * nc)
+    keyed = to_keyed(windows)
+    keyed = [keyed[2 * m * tokens : 2 * (m + 1) * tokens] for m in range(members)]
+    finish(inner, residual(inner), ask(owns), keyed, inner_bias)
+
+    owns = [joined(late, edge, m) for m in range(members)]
+    sides = [
+        joined(left, edge, m) * mc + joined(right, edge, m) * nc for m in range(members)
+    ]
+    beyonds = [whole(corner, m) for m in range(members)]
+    known = to_keyed(owns + sides + beyonds)
+    edge_asked = ask(owns)
+    edge_x = residual(edge)
+    mr2, nr2 = [jnp.concatenate([mask, mask], axis=1) for mask in (mr, nr)]
+    mc2, nc2 = [jnp.concatenate([mask, mask], axis=1) for mask in (mc, nc)]
+
+    def piece_of(array, index):
+        return array[index * tokens : (index + 1) * tokens]
+
+    middles = []
+    for m in range(members):
+        own, beyond = piece_of(known, m), piece_of(known, 2 * members + m)
+        middles.append((beyond * mr2 + own * nr2, own * mr2 + beyond * nr2))
     for half in range(2):
         arrived(corner_right.at[half], c_recv.at[0, half])
         arrived(corner_left.at[half], c_recv.at[1, half])
-    windows = []
+    fars = to_keyed(
+        [whole(corner_left, m) * mc + whole(corner_right, m) * nc for m in range(members)]
+    )
+    keyed = []
     for m in range(members):
-        own = joined(late, edge, m)
-        beyond = whole(corner, m)
-        side = joined(left, edge, m) * mc + joined(right, edge, m) * nc
-        far = whole(corner_left, m) * mc + whole(corner_right, m) * nc
+        side, far = piece_of(known, members + m), piece_of(fars, m)
         group = []
-        for middle, flank in (
-            (beyond * mr + own * nr, far * mr + side * nr),
-            (own * mr + beyond * nr, side * mr + far * nr),
+        for middle, flank in zip(
+            middles[m], (far * mr2 + side * nr2, side * mr2 + far * nr2)
         ):
-            group.append(flank * mc + middle * nc)
-            group.append(middle * mc + flank * nc)
-        windows.append(group)
-    finish(edge, windows, edge_bias)
+            group.append(flank * mc2 + middle * nc2)
+            group.append(middle * mc2 + flank * nc2)
+        keyed.append(stacked(group))
+    finish(edge, edge_x, edge_asked, keyed, edge_bias)
 
     for b in range(2):
         spots = []

time: 35.1 us -> 35.7 us (1.017); the launches traced: 34.4 us -> 35.6 us
  Pallas kernels: 33.7 us -> 34.9 us
    pallas_call x1, Pallas kernels: 33.7 us -> 34.9 us  [per_device(): pl.pallas_call(functools.partial(kernel, sizes), out_shape=pltpu.VMEM(fie...]
where the time goes in v4:
time: 35.7 us; the launch traced here: 35.6 us
  Pallas kernels  34.9 us (98%)
  local copies, waits for them, and re-layouts  0.68 us (2%)
    pallas_call x1, Pallas kernels, per_device(): pl.pallas_call(functools.partial(kernel, sizes), out_shape=pltpu.VMEM(fie...  34.9 us

profile of v4, /device:TPU:1, one launch (start us, length us, event | category | flops | bytes accessed | tf_op | source)
XLA Modules:
  0.0 35.6 jit_solution(8575270467060497023)
XLA Ops:
  0.0 34.9 %scorer.1 = bf16[3,16,8,256]{3,2,1,0:T(8,128)(2,1)S(1)} custom-call(bf16[3,16,8,256]{3,2,1,0:T(8,128)(2,1)} %h_fields.1, s32[8,16]{1,0:T(8,128)} %bitcast.2, s32[2]{0:T(128)} %offsets.1, f32[1,256]{1,0:T(1,128)} %bitcast.3, bf16[256,768]{1,0:T(8,128)(2,1)} %h_win_qkv.1, bf16[256,256]{1,0:T(8,128)(2,1)} %h_win_out.1, bf16[256,1024]{1,0:T(8,128)(2,1)} %h_win_up.1, ...), custom_call_target="tpu_custom_call" | custom-call | tf_op jit(solution)/shard_map/scorer/pallas_call | solution.py:446
  34.9 0.7 %copy.16 = bf16[3,16,8,256]{3,2,1,0:T(8,128)(2,1)} copy(bf16[3,16,8,256]{3,2,1,0:T(8,128)(2,1)S(1)} %scorer.1) | data formatting | bytes 393216

commit v5 on v4

--- a/solution.py
+++ b/solution.py
@@ -180,20 +180,19 @@
 
     sends = {}
 
-    def send_members(block):
-        for i, (half, peer) in enumerate(
-            ((other, mate), (other, far_other), (core, far_same))
-        ):
-            sends[i, block] = push(
-                mine.at[block, half], got.at[i, block], a_send.at[i, block],
-                a_recv.at[i, block], peer,
-            )
-
-    window_section(0, True)
+    def send_members(block, i, peer):
+        for half in range(2):
+            sends[i, half] = push(
+                mine.at[block, half], got.at[i, half], a_send.at[i, half],
+                a_recv.at[i, half], peer,
+            )
+
+    window_section(other, True)
     pl.semaphore_wait(barrier, 7)
-    send_members(0)
-    window_section(1, False)
-    send_members(1)
+    send_members(other, 1, far_other)
+    send_members(other, 0, mate)
+    window_section(core, False)
+    send_members(core, 2, far_same)
     loads[5].wait()
     loads[6].wait()
 
@@ -212,7 +211,7 @@
         ).reshape(members, part, -1)
 
     def member_attention(e):
-        member_qkv(0, mine[e, core], True)
+        member_qkv(0, mine[core, e], True)
         sends[0, e].wait_recv()
         member_qkv(1, got[0, e], True)
         for i in (1, 2):
@@ -254,13 +253,14 @@
     def arrived(buffer, sem):
         pltpu.make_async_copy(buffer, buffer, sem).wait()
 
-    for block in range(2):
-        member_attention(block)
-        member_add(block, core, mixed[0].astype(BF))
-        send_halo(block, core)
-        arrived(mixed_got.at[block], r_recv.at[block])
-        member_add(block, other, mixed_got[block])
-        send_halo(block, other)
+    for half in range(2):
+        member_attention(half)
+        member_add(core, half, mixed[0].astype(BF))
+        send_halo(core, half)
+    for half in range(2):
+        arrived(mixed_got.at[half], r_recv.at[half])
+        member_add(other, half, mixed_got[half])
+        send_halo(other, half)
 
     mr, nr = row_low.astype(BF), (1.0 - row_low).astype(BF)
     mc, nc = col_low.astype(BF), (1.0 - col_low).astype(BF)
@@ -281,8 +281,8 @@
                  c_recv.at[1, half], lon_right)
         )
 
-    relay(core)
-    relay(other)
+    relay(0)
+    relay(1)
 
     q_tok = lax.broadcasted_iota(jnp.int32, (tokens, 4 * tokens), 0)
     k_tok = lax.broadcasted_iota(jnp.int32, (tokens, 4 * tokens), 1)

time: 35.7 us -> 34.7 us (0.972); the launches traced: 35.6 us -> 34.1 us
  Pallas kernels: 34.9 us -> 33.4 us
    pallas_call x1, Pallas kernels: 34.9 us -> 33.4 us  [per_device(): pl.pallas_call(functools.partial(kernel, sizes), out_shape=pltpu.VMEM(fie...]
where the time goes in v5:
time: 34.7 us; the launch traced here: 34.1 us
  Pallas kernels  33.4 us (96%)
  local copies, waits for them, and re-layouts  0.68 us (2%)
    pallas_call x1, Pallas kernels, per_device(): pl.pallas_call(functools.partial(kernel, sizes), out_shape=pltpu.VMEM(fie...  33.4 us

profile of v5, /device:TPU:1, one launch (start us, length us, event | category | flops | bytes accessed | tf_op | source)
XLA Modules:
  0.0 34.1 jit_solution(17973949621848386046)
XLA Ops:
  0.0 33.4 %scorer.1 = bf16[3,16,8,256]{3,2,1,0:T(8,128)(2,1)S(1)} custom-call(bf16[3,16,8,256]{3,2,1,0:T(8,128)(2,1)} %h_fields.1, s32[8,16]{1,0:T(8,128)} %bitcast.2, s32[2]{0:T(128)} %offsets.1, f32[1,256]{1,0:T(1,128)} %bitcast.3, bf16[256,768]{1,0:T(8,128)(2,1)} %h_win_qkv.1, bf16[256,256]{1,0:T(8,128)(2,1)} %h_win_out.1, bf16[256,1024]{1,0:T(8,128)(2,1)} %h_win_up.1, ...), custom_call_target="tpu_custom_call" | custom-call | tf_op jit(solution)/shard_map/scorer/pallas_call | solution.py:446
  33.4 0.7 %copy.16 = bf16[3,16,8,256]{3,2,1,0:T(8,128)(2,1)} copy(bf16[3,16,8,256]{3,2,1,0:T(8,128)(2,1)S(1)} %scorer.1) | data formatting | bytes 393216

commit v6 on v5

--- a/solution.py
+++ b/solution.py
@@ -253,9 +253,12 @@
     def arrived(buffer, sem):
         pltpu.make_async_copy(buffer, buffer, sem).wait()
 
+    kept = []
     for half in range(2):
         member_attention(half)
-        member_add(core, half, mixed[0].astype(BF))
+        kept.append(mixed[0].astype(BF))
+    for half in range(2):
+        member_add(core, half, kept[half])
         send_halo(core, half)
     for half in range(2):
         arrived(mixed_got.at[half], r_recv.at[half])

time: 34.7 us -> 35.1 us (1.012)
  Pallas kernels: 33.4 us -> 33.9 us
    pallas_call x1, Pallas kernels: 33.4 us -> 33.9 us  [per_device(): pl.pallas_call(functools.partial(kernel, sizes), out_shape=pltpu.VMEM(fie...]
where the time goes in v6:
time: 35.1 us; the launch traced here: 34.6 us
  Pallas kernels  33.9 us (97%)
  local copies, waits for them, and re-layouts  0.68 us (2%)
    pallas_call x1, Pallas kernels, per_device(): pl.pallas_call(functools.partial(kernel, sizes), out_shape=pltpu.VMEM(fie...  33.9 us

profile of v6, /device:TPU:1, one launch (start us, length us, event | category | flops | bytes accessed | tf_op | source)
XLA Modules:
  0.0 34.6 jit_solution(236291411310719819)
XLA Ops:
  0.0 33.9 %scorer.1 = bf16[3,16,8,256]{3,2,1,0:T(8,128)(2,1)S(1)} custom-call(bf16[3,16,8,256]{3,2,1,0:T(8,128)(2,1)} %h_fields.1, s32[8,16]{1,0:T(8,128)} %bitcast.2, s32[2]{0:T(128)} %offsets.1, f32[1,256]{1,0:T(1,128)} %bitcast.3, bf16[256,768]{1,0:T(8,128)(2,1)} %h_win_qkv.1, bf16[256,256]{1,0:T(8,128)(2,1)} %h_win_out.1, bf16[256,1024]{1,0:T(8,128)(2,1)} %h_win_up.1, ...), custom_call_target="tpu_custom_call" | custom-call | tf_op jit(solution)/shard_map/scorer/pallas_call | solution.py:449
  33.9 0.7 %copy.16 = bf16[3,16,8,256]{3,2,1,0:T(8,128)(2,1)} copy(bf16[3,16,8,256]{3,2,1,0:T(8,128)(2,1)S(1)} %scorer.1) | data formatting | bytes 393216
